TPU v7x, 32 devices: a whole 2x2x4 slice. The times are simulated.
32 devices in a mesh: dp: 8 (over y, x, core), tensor: 4 (over z).
Axes of the slice: x: 2, y: 2, z: 4, core: 2. Of those that a mesh axis runs over, the one named last changes fastest.
Arguments:
- layer_input: bfloat16 [8192, 768], P(('dp', 'tensor')), may hold values from -12 to 12
- attn_gain: float32 [768], replicated, may hold values from 0.5 to 1.5
- query_weight: bfloat16 [768, 768], P(None, 'tensor'), may hold values from -0.21875 to 0.21875
- key_weight: bfloat16 [768, 768], P(None, 'tensor'), may hold values from -0.21875 to 0.21875
- value_weight: bfloat16 [768, 768], P(None, 'tensor'), may hold values from -0.21875 to 0.21875
- out_weight: bfloat16 [768, 768], P('tensor'), may hold values from -3 to 3
- moe_gain: float32 [768], replicated, may hold values from 0.5 to 1.5
- router_weight: float32 [768, 12], replicated, may hold values from -0.109375 to 0.109375
- gate_residual: float32 [8192, 12], P('dp'), may hold values from -3 to 3
- const_gate: float32 [2, 768, 2], replicated, may hold values from -0.21875 to 0.21875
- const_value: float32 [2, 768], replicated, may hold values from -6 to 6
- gate_weight: bfloat16 [8, 768, 2048], P(None, None, 'tensor'), may hold values from -0.21875 to 0.21875
- up_weight: bfloat16 [8, 768, 2048], P(None, None, 'tensor'), may hold values from -0.21875 to 0.21875
- down_weight: bfloat16 [8, 2048, 768], P(None, 'tensor'), may hold values from -0.75 to 0.75
- routes: int32 [8192, 2], P('dp'), may hold values from 0 to 11, all different within a row; in each aligned block of 1024 rows (0 to 1023, 1024 to 2047, ...) at most 256 rows name the same one
- grad_out: bfloat16 [8192, 768], P(('dp', 'tensor')), may hold values from -12 to 12
Outputs:
- output: bfloat16 [8192, 768], P(('dp', 'tensor'))
- input_grad: bfloat16 [8192, 768], P(('dp', 'tensor'))
- attn_gain_grad: float32 [768], replicated
- query_grad: float32 [768, 768], P('dp', 'tensor')
- key_grad: float32 [768, 768], P('dp', 'tensor')
- value_grad: float32 [768, 768], P('dp', 'tensor')
- out_grad: float32 [768, 768], P('tensor', 'dp')
- moe_gain_grad: float32 [768], replicated
- router_grad: float32 [768, 12], replicated
- const_gate_grad: float32 [2, 768, 2], replicated
- const_value_grad: float32 [2, 768], replicated
- gate_grad: float32 [8, 768, 2048], P(None, 'dp', 'tensor')
- up_grad: float32 [8, 768, 2048], P(None, 'dp', 'tensor')
- down_grad: float32 [8, 2048, 768], P(None, 'tensor', 'dp')
Inputs may be any that keep to these rules, and one draw needn't show every extreme that they name: `routes`: in each aligned block of 1024 rows (the tokens of one index of dp) every expert number is named by at most 256 rows, a bound that some block reaches; the two numbers of a row differ.
All inputs are finite; a program needn't handle non-finite values.
Results may differ from a plain program's by a relative error of at most 0.024.
Values may be sent and summed in bfloat16 or wider, within the bound.
A program may use at most 256 MiB of HBM per device.

v0:
```python
import math

import jax
import jax.numpy as jnp
from jax import lax
from jax.sharding import PartitionSpec as P

HD = 64
LENGTH = 1024
BLOCK = 256
CAP = 256


EPSILON = 1e-06
MASKED = -1e30


def rope_tables(length, head_width):
    position = jnp.arange(length, dtype=jnp.float32)[:, None]
    inverse = jnp.exp(
        jnp.arange(head_width // 2, dtype=jnp.float32) * (-2.0 * math.log(10000.0) / head_width)
    )
    angle = position * inverse[None, :]
    return (jnp.cos(angle), jnp.sin(angle))


def rotate(values, cosine, sine):
    half_width = values.shape[-1] // 2
    first_half = values[..., :half_width]
    second_half = values[..., half_width:]
    cos_table = cosine[:, None, :]
    sin_table = sine[:, None, :]
    return jnp.concatenate(
        [
            first_half * cos_table - second_half * sin_table,
            second_half * cos_table + first_half * sin_table,
        ],
        axis=-1,
    )


def unrotate(values, cosine, sine):
    half_width = values.shape[-1] // 2
    first_half = values[..., :half_width]
    second_half = values[..., half_width:]
    cos_table = cosine[:, None, :]
    sin_table = sine[:, None, :]
    return jnp.concatenate(
        [
            first_half * cos_table + second_half * sin_table,
            second_half * cos_table - first_half * sin_table,
        ],
        axis=-1,
    )


def rms_norm(values, gain):
    scale = lax.rsqrt(jnp.mean(values * values, axis=-1, keepdims=True) + EPSILON)
    return values * scale * gain


def block_mask(query_start, query_rows, length):
    query_pos = query_start + jnp.arange(query_rows, dtype=jnp.int32)
    key_pos = jnp.arange(length, dtype=jnp.int32)
    return (key_pos // BLOCK)[None, :] <= (query_pos // BLOCK)[:, None]


def side_experts(norm_values, router_w, mix_weight, const_rows, residual_logits, picks, ffn_count):
    logits = jnp.dot(norm_values, router_w, precision=lax.Precision.HIGHEST) + residual_logits
    soft_probs = jax.nn.softmax(logits, axis=-1)
    chosen = jnp.take_along_axis(soft_probs, picks, axis=1)
    mixing = jax.nn.softmax(
        jnp.einsum("rd,cdj->rcj", norm_values, mix_weight, precision=lax.Precision.HIGHEST), axis=-1
    )
    constant = (
        mixing[..., 0:1] * norm_values[:, None, :] + mixing[..., 1:2] * const_rows[None, :, :]
    )
    special = (picks == ffn_count + 1).astype(jnp.float32)[..., None] * norm_values[:, None, :]
    special = (
        special
        + (picks == ffn_count + 2).astype(jnp.float32)[..., None] * constant[:, 0][:, None, :]
    )
    special = (
        special
        + (picks == ffn_count + 3).astype(jnp.float32)[..., None] * constant[:, 1][:, None, :]
    )
    return (chosen, jnp.sum(chosen[..., None] * special, axis=1))


def attention_forward(query, key, value):
    seq_count, length, head_count, head_width = query.shape
    query_rows = min(512, length)
    block_count = length // query_rows
    scale = head_width ** (-0.5)

    def one_block(block_index):
        seq_index = block_index // block_count
        query_start = block_index % block_count * query_rows
        query_seq = lax.dynamic_index_in_dim(query, seq_index, 0, keepdims=False)
        query_blk = lax.dynamic_slice_in_dim(query_seq, query_start, query_rows, 0)
        key_seq = lax.dynamic_index_in_dim(key, seq_index, 0, keepdims=False)
        value_seq = lax.dynamic_index_in_dim(value, seq_index, 0, keepdims=False)
        scores = (
            jnp.einsum("qhd,khd->hqk", query_blk, key_seq, preferred_element_type=jnp.float32)
            * scale
        )
        scores = jnp.where(block_mask(query_start, query_rows, length)[None], scores, MASKED)
        row_max = jnp.max(scores, axis=-1, keepdims=True)
        exp_scores = jnp.exp(scores - row_max)
        row_total = jnp.sum(exp_scores, axis=-1, keepdims=True)
        soft_probs = (exp_scores / row_total).astype(jnp.bfloat16)
        result = jnp.einsum(
            "hqk,khd->qhd", soft_probs, value_seq, preferred_element_type=jnp.float32
        )
        return (result, (row_max + jnp.log(row_total))[..., 0])

    return lax.map(one_block, jnp.arange(seq_count * block_count, dtype=jnp.int32))


def attention_backward(query, key, value, grad_mixed, log_totals):
    seq_count, length, head_count, head_width = query.shape
    query_rows = min(512, length)
    block_count = length // query_rows
    scale = head_width ** (-0.5)
    log_totals = log_totals.reshape(seq_count, block_count, head_count, query_rows)

    def per_sequence(operands):
        query_seq, key_seq, value_seq, grad_seq, total_seq = operands

        def block_step(carried, block_index):
            key_acc, value_acc = carried
            query_start = block_index * query_rows
            query_blk = lax.dynamic_slice_in_dim(query_seq, query_start, query_rows, 0)
            grad_blk = lax.dynamic_slice_in_dim(grad_seq, query_start, query_rows, 0)
            total_blk = lax.dynamic_index_in_dim(total_seq, block_index, 0, keepdims=False)
            scores = (
                jnp.einsum("qhd,khd->hqk", query_blk, key_seq, preferred_element_type=jnp.float32)
                * scale
            )
            scores = jnp.where(block_mask(query_start, query_rows, length)[None], scores, MASKED)
            soft_probs = jnp.exp(scores - total_blk[..., None])
            grad_probs = jnp.einsum(
                "qhd,khd->hqk", grad_blk, value_seq, preferred_element_type=jnp.float32
            )
            grad_scores = (
                soft_probs * (grad_probs - jnp.sum(soft_probs * grad_probs, axis=-1, keepdims=True))
            ).astype(jnp.bfloat16)
            query_part = (
                jnp.einsum("hqk,khd->qhd", grad_scores, key_seq, preferred_element_type=jnp.float32)
                * scale
            )
            key_acc = (
                key_acc
                + jnp.einsum(
                    "hqk,qhd->khd", grad_scores, query_blk, preferred_element_type=jnp.float32
                )
                * scale
            )
            value_acc = value_acc + jnp.einsum(
                "hqk,qhd->khd",
                soft_probs.astype(jnp.bfloat16),
                grad_blk,
                preferred_element_type=jnp.float32,
            )
            return ((key_acc, value_acc), query_part)

        zero_acc = jnp.zeros((length, head_count, head_width), jnp.float32)
        (key_acc, value_acc), query_parts = lax.scan(
            block_step, (zero_acc, zero_acc), jnp.arange(block_count, dtype=jnp.int32)
        )
        return (query_parts.reshape(length, head_count, head_width), key_acc, value_acc)

    return lax.map(per_sequence, (query, key, value, grad_mixed, log_totals))


def on_device(
    layer_input,
    attn_gain,
    query_weight,
    key_weight,
    value_weight,
    out_weight,
    moe_gain,
    router_weight,
    gate_residual,
    const_gate,
    const_value,
    gate_weight,
    up_weight,
    down_weight,
    routes,
    grad_out,
):
    local_rows, model_width = layer_input.shape
    tensor_size = lax.axis_size("tensor")
    group_rows = local_rows * tensor_size
    row_start = lax.axis_index("tensor") * local_rows
    seq_count = group_rows // LENGTH
    head_count = query_weight.shape[1] // HD
    ffn_count = gate_weight.shape[0]
    route_count = router_weight.shape[1]
    slot_count = ffn_count * CAP
    cosine, sine = rope_tables(LENGTH, HD)
    input_wide = layer_input.astype(jnp.float32)
    norm_attn, pull_attn_norm = jax.vjp(rms_norm, input_wide, attn_gain)
    norm_attn = norm_attn.astype(jnp.bfloat16)
    attn_rows = lax.all_gather(norm_attn, "tensor", axis=0, tiled=True)
    query_raw = jnp.dot(attn_rows, query_weight, preferred_element_type=jnp.float32).reshape(
        seq_count, LENGTH, head_count, HD
    )
    key_raw = jnp.dot(attn_rows, key_weight, preferred_element_type=jnp.float32).reshape(
        seq_count, LENGTH, head_count, HD
    )
    value_raw = jnp.dot(attn_rows, value_weight, preferred_element_type=jnp.float32).reshape(
        seq_count, LENGTH, head_count, HD
    )
    query = rotate(query_raw, cosine, sine).astype(jnp.bfloat16)
    key = rotate(key_raw, cosine, sine).astype(jnp.bfloat16)
    value = value_raw.astype(jnp.bfloat16)
    mixed, log_totals = attention_forward(query, key, value)
    mixed = mixed.reshape(group_rows, head_count * HD).astype(jnp.bfloat16)
    attn_part = jnp.dot(mixed, out_weight, preferred_element_type=jnp.float32)
    attn_sum = lax.psum_scatter(
        attn_part.astype(jnp.bfloat16), "tensor", scatter_dimension=0, tiled=True
    ).astype(jnp.float32)
    hidden = input_wide + attn_sum
    norm_moe, pull_moe_norm = jax.vjp(rms_norm, hidden, moe_gain)
    norm_moe = norm_moe.astype(jnp.bfloat16)
    moe_rows = lax.all_gather(norm_moe, "tensor", axis=0, tiled=True)
    logits = (
        jnp.dot(moe_rows.astype(jnp.float32), router_weight, precision=lax.Precision.HIGHEST)
        + gate_residual
    )
    chosen = jnp.take_along_axis(jax.nn.softmax(logits, axis=-1), routes, axis=1)
    flat_routes = routes.reshape(-1)
    onehot = (flat_routes[:, None] == jnp.arange(route_count, dtype=jnp.int32)[None, :]).astype(
        jnp.int32
    )
    earlier = jnp.cumsum(onehot, axis=0) - onehot
    slot_rank = jnp.sum(onehot * earlier, axis=1)
    is_ffn = flat_routes < ffn_count
    slot_index = jnp.where(is_ffn, flat_routes * CAP + slot_rank, slot_count)
    pair_slot = slot_index.reshape(group_rows, 2)
    slot_ids = jnp.arange(slot_count, dtype=jnp.int32)[:, None]
    dispatch = (
        (pair_slot[:, 0][None, :] == slot_ids) | (pair_slot[:, 1][None, :] == slot_ids)
    ).astype(jnp.bfloat16)
    expert_in = (
        jnp.dot(dispatch, moe_rows, preferred_element_type=jnp.float32)
        .astype(jnp.bfloat16)
        .reshape(ffn_count, CAP, model_width)
    )
    gate_pre = jnp.einsum(
        "ecd,edf->ecf", expert_in, gate_weight, preferred_element_type=jnp.float32
    )
    up_pre = jnp.einsum("ecd,edf->ecf", expert_in, up_weight, preferred_element_type=jnp.float32)
    active = (jax.nn.silu(gate_pre) * up_pre).astype(jnp.bfloat16)
    expert_part = jnp.einsum(
        "ecf,efd->ecd", active, down_weight, preferred_element_type=jnp.float32
    )
    padded = jnp.concatenate(
        [expert_part.reshape(slot_count, model_width), jnp.zeros((1, model_width), jnp.float32)],
        axis=0,
    )
    picked = padded[slot_index].reshape(group_rows, 2, model_width)
    ffn_part = jnp.sum(chosen[..., None] * picked, axis=1)
    ffn_sum = lax.psum_scatter(
        ffn_part.astype(jnp.bfloat16), "tensor", scatter_dimension=0, tiled=True
    ).astype(jnp.float32)
    local_routes = lax.dynamic_slice_in_dim(routes, row_start, local_rows, 0)
    local_logits = lax.dynamic_slice_in_dim(gate_residual, row_start, local_rows, 0)

    def side_local(norm_values, router_w, mix_weight, const_rows):
        return side_experts(
            norm_values, router_w, mix_weight, const_rows, local_logits, local_routes, ffn_count
        )

    (local_chosen, special_sum), pull_side = jax.vjp(
        side_local, norm_moe.astype(jnp.float32), router_weight, const_gate, const_value
    )
    output = (hidden + ffn_sum + special_sum).astype(jnp.bfloat16)
    grad_wide = grad_out.astype(jnp.float32)
    grad_rows = lax.all_gather(grad_out, "tensor", axis=0, tiled=True)
    owner_index = (
        jnp.zeros((slot_count + 1,), jnp.int32)
        .at[slot_index]
        .set(jnp.repeat(jnp.arange(group_rows, dtype=jnp.int32), 2))
    )
    slot_weight = (
        jnp.zeros((slot_count + 1,), jnp.float32)
        .at[slot_index]
        .add(jnp.where(is_ffn, chosen.reshape(-1), 0.0))
    )
    grad_expert = (
        (grad_rows[owner_index[:slot_count]].astype(jnp.float32) * slot_weight[:slot_count, None])
        .astype(jnp.bfloat16)
        .reshape(ffn_count, CAP, model_width)
    )
    chosen_part = jnp.sum(grad_rows.astype(jnp.float32)[:, None, :] * picked, axis=-1)
    grad_active = jnp.einsum(
        "ecd,efd->ecf", grad_expert, down_weight, preferred_element_type=jnp.float32
    )
    sigmoid_gate = jax.nn.sigmoid(gate_pre)
    grad_gate = (
        grad_active * up_pre * sigmoid_gate * (1.0 + gate_pre * (1.0 - sigmoid_gate))
    ).astype(jnp.bfloat16)
    grad_up = (grad_active * gate_pre * sigmoid_gate).astype(jnp.bfloat16)
    grad_in_expert = jnp.einsum(
        "ecf,edf->ecd", grad_gate, gate_weight, preferred_element_type=jnp.float32
    ) + jnp.einsum("ecf,edf->ecd", grad_up, up_weight, preferred_element_type=jnp.float32)
    down_part = jnp.einsum("ecf,ecd->efd", active, grad_expert, preferred_element_type=jnp.float32)
    gate_part = jnp.einsum("ecd,ecf->edf", expert_in, grad_gate, preferred_element_type=jnp.float32)
    up_part = jnp.einsum("ecd,ecf->edf", expert_in, grad_up, preferred_element_type=jnp.float32)
    padded_grad = jnp.concatenate(
        [grad_in_expert.reshape(slot_count, model_width), jnp.zeros((1, model_width), jnp.float32)],
        axis=0,
    )
    ffn_back = jnp.sum(padded_grad[slot_index].reshape(group_rows, 2, model_width), axis=1)
    moe_back, chosen_back = (
        lax.psum_scatter(
            ffn_back.astype(jnp.bfloat16), "tensor", scatter_dimension=0, tiled=True
        ).astype(jnp.float32),
        lax.psum_scatter(
            chosen_part.astype(jnp.bfloat16), "tensor", scatter_dimension=0, tiled=True
        ).astype(jnp.float32),
    )
    side_back, router_part, const_gate_part, const_value_part = pull_side((chosen_back, grad_wide))
    hidden_norm_back, moe_gain_part = pull_moe_norm(moe_back + side_back)
    hidden_grad = grad_wide + hidden_norm_back
    attn_grad_rows = lax.all_gather(hidden_grad.astype(jnp.bfloat16), "tensor", axis=0, tiled=True)
    out_part = jnp.einsum("gh,gd->hd", mixed, attn_grad_rows, preferred_element_type=jnp.float32)
    grad_mixed = (
        jnp.einsum("gd,hd->gh", attn_grad_rows, out_weight, preferred_element_type=jnp.float32)
        .astype(jnp.bfloat16)
        .reshape(seq_count, LENGTH, head_count, HD)
    )
    query_back, key_back, value_back = attention_backward(query, key, value, grad_mixed, log_totals)
    query_back = (
        unrotate(query_back, cosine, sine).astype(jnp.bfloat16).reshape(group_rows, head_count * HD)
    )
    key_back = (
        unrotate(key_back, cosine, sine).astype(jnp.bfloat16).reshape(group_rows, head_count * HD)
    )
    value_back = value_back.astype(jnp.bfloat16).reshape(group_rows, head_count * HD)
    query_part = jnp.einsum("gd,gh->dh", attn_rows, query_back, preferred_element_type=jnp.float32)
    key_part = jnp.einsum("gd,gh->dh", attn_rows, key_back, preferred_element_type=jnp.float32)
    value_part = jnp.einsum("gd,gh->dh", attn_rows, value_back, preferred_element_type=jnp.float32)
    attn_back = jnp.einsum(
        "gh,dh->gd", query_back, query_weight, preferred_element_type=jnp.float32
    )
    attn_back = attn_back + jnp.einsum(
        "gh,dh->gd", key_back, key_weight, preferred_element_type=jnp.float32
    )
    attn_back = attn_back + jnp.einsum(
        "gh,dh->gd", value_back, value_weight, preferred_element_type=jnp.float32
    )
    norm_back = lax.psum_scatter(
        attn_back.astype(jnp.bfloat16), "tensor", scatter_dimension=0, tiled=True
    ).astype(jnp.float32)
    input_norm_back, attn_gain_part = pull_attn_norm(norm_back)
    input_grad = (hidden_grad + input_norm_back).astype(jnp.bfloat16)
    small_sums = lax.psum(
        (attn_gain_part, moe_gain_part, router_part, const_gate_part, const_value_part),
        ("dp", "tensor"),
    )
    weight_sums = (
        lax.psum_scatter(query_part, "dp", scatter_dimension=0, tiled=True),
        lax.psum_scatter(key_part, "dp", scatter_dimension=0, tiled=True),
        lax.psum_scatter(value_part, "dp", scatter_dimension=0, tiled=True),
        lax.psum_scatter(out_part, "dp", scatter_dimension=1, tiled=True),
        lax.psum_scatter(gate_part, "dp", scatter_dimension=1, tiled=True),
        lax.psum_scatter(up_part, "dp", scatter_dimension=1, tiled=True),
        lax.psum_scatter(down_part, "dp", scatter_dimension=2, tiled=True),
    )
    return (
        output,
        input_grad,
        small_sums[0],
        weight_sums[0],
        weight_sums[1],
        weight_sums[2],
        weight_sums[3],
        small_sums[1],
        small_sums[2],
        small_sums[3],
        small_sums[4],
        weight_sums[4],
        weight_sums[5],
        weight_sums[6],
    )


def solution(mesh):
    in_specs = (
        P(("dp", "tensor"), None),
        P(),
        P(None, "tensor"),
        P(None, "tensor"),
        P(None, "tensor"),
        P("tensor", None),
        P(),
        P(),
        P("dp", None),
        P(),
        P(),
        P(None, None, "tensor"),
        P(None, None, "tensor"),
        P(None, "tensor", None),
        P("dp", None),
        P(("dp", "tensor"), None),
    )
    out_specs = (
        P(("dp", "tensor"), None),
        P(("dp", "tensor"), None),
        P(),
        P("dp", "tensor"),
        P("dp", "tensor"),
        P("dp", "tensor"),
        P("tensor", "dp"),
        P(),
        P(),
        P(),
        P(),
        P(None, "dp", "tensor"),
        P(None, "dp", "tensor"),
        P(None, "tensor", "dp"),
    )
    return jax.shard_map(
        on_device, mesh=mesh, in_specs=in_specs, out_specs=out_specs, check_vma=False
    )
```

profile of v0, /device:TPU:0, one launch (start us, length us, event | category | flops | bytes accessed | tf_op | source)
XLA Modules:
  0.0 1013.8 jit_solution(8574953001527332081)
XLA Ops:
  12.2 39.3 %all-gather.5.cloned.1.call-done = bf16[1024,768]{1,0:T(8,128)(2,1)} async-done(((bf16[256,768]{1,0:T(8,128)(2,1)}), bf16[1024,768]{1,0:T(8,128)(2,1)}) %all-gather.5.cloned.1.call-update) | async-done | bytes 1572880 | tf_op jit(solution)/shard_map/all_gather | solution.py:207
  51.5 2.1 fusion.105
  53.6 2.2 fusion.106
  57.6 16.8 %while.44 = (s32[]{:T(128)}, bf16[2,512,3,64]{1,3,2,0:T(8,128)(2,1)S(1)}, f32[2,3,512]{2,1,0:T(4,128)S(1)}, s32[2]{0:T(128)S(1)}, bf16[1,1024,3,64]{1,3,2,0:T(8,...) while((s32[]{:T(128)}, ...), condition=%wide.region_4.5_spmd, body=%wide.region_1.4_spmd.sunk | while | flops 422066688 | bytes 22419756 | solution.py:117
  63.8 2.2 fusion.193
  72.1 2.2 fusion.193
  78.3 3.4 reduce-window.6
  82.5 28.5 %reduce-scatter.17.cloned.1.call-done = bf16[256,768]{1,0:T(8,128)(2,1)} async-done(((bf16[1024,768]{1,0:T(8,128)(2,1)}), bf16[256,768]{1,0:T(8,128)(2,1)}) %reduce-scatter.17.cloned.1.call-update) | async-done | bytes 393232 | tf_op jit(solution)/shard_map/reduce_scatter | solution.py:223
  112.2 2.2 fusion.100
  119.0 8.1 scatter_custom_fusion
  129.4 19.3 %all-gather.9.cloned.1.call-done = bf16[1024,768]{1,0:T(8,128)(2,1)} async-done(((bf16[256,768]{1,0:T(8,128)(2,1)}), bf16[1024,768]{1,0:T(8,128)(2,1)}) %all-gather.9.cloned.1.call-update) | async-done | bytes 1572880 | tf_op jit(solution)/shard_map/all_gather | solution.py:283
  148.7 11.7 %gather_fusion.1 = bf16[2048,768]{1,0:T(8,128)(2,1)} fusion(bf16[1024,768]{1,0:T(8,128)(2,1)} %all-gather.9.cloned.1.call-done, s32[2048]{0:T(1024)S(1)} %fusion.89), kind=kCustom, calls=%fused_computation.1 | custom fusion | bytes 6299648 | tf_op jit(solution)/shard_map/gather | solution.py:295
  160.4 5.5 copy.149
  169.5 4.5 gather_fusion.4
  175.9 10.8 %all-gather.7.cloned.1.call-done = bf16[1024,768]{1,0:T(8,128)(2,1)} async-done(((bf16[256,768]{1,0:T(8,128)(2,1)}), bf16[1024,768]{1,0:T(8,128)(2,1)}) %all-gather.7.cloned.1.call-update) | async-done | bytes 1572880 | tf_op jit(solution)/shard_map/all_gather | solution.py:229
  186.7 2.7 fusion.104
  189.6 16.8 %gather_fusion.3 = f32[2048]{0:T(1024)S(1)} fusion(f32[1024,12]{0,1:T(8,128)S(1)} %fusion.85, s32[2048]{0:T(1024)S(1)} %reshape.630), kind=kCustom, calls=%fused_computation.3 | custom fusion | bytes 32768 | tf_op jit(solution)/shard_map/jit(take_along_axis)/gather | solution.py:234
  207.6 11.9 %scatter_custom_fusion.1 = f32[2049]{0:T(1024)S(1)} fusion(s32[2048]{0:T(1024)} %bitcast.247, f32[2048]{0:T(1024)S(1)} %compare_select_fusion.3, f32[]{:T(128)} %constant.317.clone.1), kind=kCustom, calls=%fused_computation.206 | custom fusion | flops 2048 | bytes 8708 | tf_op jit(solution)/shard_map/scatter-add | solution.py:292
  219.6 6.0 fusion.56
  225.6 3.8 fusion.107
  229.4 6.6 fusion.108
  236.0 12.4 %multiply_convert_fusion.2 = (bf16[8,256,512]{2,1,0:T(8,128)(2,1)}, bf16[8,256,512]{2,1,0:T(8,128)(2,1)}, bf16[8,256,512]{2,1,0:T(8,128)(2,1)S(1)}) fusion(f32[8,256,512]{2,1,0:T(8,128)} %fusion.107, f32[8,256,512]{2,1,0:T(8,128)} %fusion.108, bf16[8,512,768]{2,1,0:T(8,128)(2,1)} %param.33, f32[8,256,768]{1,2,0:T(8,128)} %copy.149, f32[8,256]{1,0:T(8,128)S(1)} %mul.753), kind=kOutput, calls=%fused_computation.93 | convolution fusion | flops 1630535680 | bytes 27271168 | tf_op jit(solution)/shard_map/ecd,efd->ecf/dot_general | solution.py:300
  248.4 5.3 fusion.109
  253.8 3.1 concatenate.60
  256.8 13.5 %gather_fusion = f32[2048,768]{1,0:T(8,128)} fusion(f32[2049,768]{1,0:T(8,128)} %concatenate.60, s32[2048]{0:T(1024)S(1)} %copy-done.64), kind=kCustom, calls=%fused_computation | custom fusion | bytes 12591104 | tf_op jit(solution)/shard_map/gather | solution.py:265
  270.3 8.3 reshape.595
  278.7 17.0 %multiply_reduce_fusion.1 = (bf16[1024,2]{1,0:T(8,128)(2,1)}, bf16[1024,768]{1,0:T(8,128)(2,1)}) fusion(f32[1024,2,768]{2,1,0:T(2,128)} %reshape.595, f32[1024,768]{1,0:T(8,128)} %convert_element_type.212, f32[1024,2]{1,0:T(8,128)S(1)} %copy.141), kind=kLoop, calls=%fused_computation.90 | loop fusion | flops 5502976 | bytes 11022336 | tf_op jit(solution)/shard_map/reduce_sum | solution.py:299
  295.7 5.4 fusion.110
  301.2 3.4 convolution_add_fusion
  304.6 3.1 concatenate.61
  307.6 13.5 %gather_fusion.2 = f32[2048,768]{1,0:T(8,128)} fusion(f32[2049,768]{1,0:T(8,128)} %concatenate.61, s32[2048]{0:T(1024)S(1)} %copy-done.64), kind=kCustom, calls=%fused_computation.2 | custom fusion | bytes 12591104 | tf_op jit(solution)/shard_map/gather | solution.py:318
  321.1 8.2 reshape.599
  329.3 11.6 %reduce_sum.304 = bf16[1024,768]{1,0:T(8,128)(2,1)} reduce(f32[1024,2,768]{2,1,0:T(2,128)} %reshape.599, f32[]{:T(128)} %constant.317.clone.1), dimensions={1}, to_apply=%region_21.22 | reduce | flops 786432 | bytes 7864324 | tf_op jit(solution)/shard_map/reduce_sum | solution.py:318
  342.1 2.9 multiply_reduce_fusion.4
  348.7 25.8 %scatter_fusion = f32[256,12]{0,1:T(8,128)S(1)} fusion(f32[256,12]{0,1:T(8,128)S(1)} %broadcast_in_dim.177, s32[512]{0:T(512)S(1)} %copy-done.11, f32[512]{0:T(512)S(1)} %reshape.660), kind=kCustom, calls=%fused_computation.7 | custom fusion | flops 512 | bytes 10240 | tf_op jit(solution)/shard_map/transpose(jvp(jit(take_along_axis)))/scatter-add | solution.py:71
  375.3 2.8 multiply_reduce_fusion.9
  380.3 36.0 %all-gather.11.cloned.1.call-done = bf16[1024,768]{1,0:T(8,128)(2,1)} async-done(((bf16[256,768]{1,0:T(8,128)(2,1)}), bf16[1024,768]{1,0:T(8,128)(2,1)}) %all-gather.11.cloned.1.call-update) | async-done | bytes 1572880 | tf_op jit(solution)/shard_map/all_gather | solution.py:330
  416.3 2.1 convolution_convert_fusion.1
  418.4 68.0 %while.45 = (s32[]{:T(128)}, f32[1024,3,64]{0,2,1:T(8,128)}, f32[1024,3,64]{0,2,1:T(8,128)}, f32[2,512,3,64]{1,0,3,2:T(2,128)}, s32[2]{0:T(128)S(1)}, /*index=5*...) while((s32[]{:T(128)}, f32[1024,3,64]{0,2,1:T(8,128)}, ...), condition=%wide.region_38.39_spmd.clone, body=%wide.region_36.38_spmd.clone.sunk | while | flops 1031846400 | bytes 90497616 | solution.py:168
  419.8 3.6 fusion.203
  425.8 4.8 multiply_reduce_fusion.15
  432.5 2.1 fusion.206
  435.8 8.1 dynamic_update_slice.38
  443.9 2.5 fusion.204
  446.4 5.7 fusion.205
  453.6 3.7 fusion.203
  459.6 4.8 multiply_reduce_fusion.15
  466.3 2.1 fusion.206
  469.6 8.1 dynamic_update_slice.38
  477.6 2.8 fusion.204
  480.5 5.9 fusion.205
  488.4 3.2 convolution_bitcast_fusion
  502.7 9.7 fusion.64
  514.3 8.0 fusion.116
  522.4 8.0 fusion.117
  534.3 29.0 %reduce-scatter.23.cloned.1.call-done = bf16[256,768]{1,0:T(8,128)(2,1)} async-done(((bf16[1024,768]{1,0:T(8,128)(2,1)}), bf16[256,768]{1,0:T(8,128)(2,1)}) %reduce-scatter.23.cloned.1.call-update) | async-done | bytes 393232 | tf_op jit(solution)/shard_map/reduce_scatter | solution.py:357
  564.7 43.9 %all-reduce.6 = (f32[768]{0:T(1024)}, f32[768]{0:T(1024)}, f32[768,12]{0,1:T(8,128)}, f32[2,768,2]{1,2,0:T(2,128)}, f32[2,768]{1,0:T(2,128)}) all-reduce(f32[768]{0:T(1024)S(1)} %get-tuple-element.367, f32[768]{0:T(1024)} %get-tuple-element.362, f32[768,12]{0,1:T(8,128)S(1)} %fusion.98, ...), channel_id=1, replica_groups=mesh['dp'=8,'tensor'=4] {'dp','tensor'}, use_global_device_ids=true, to_apply=%region_42.43 | all-reduce | flops 15360 | bytes 122880 | tf_op jit(solution)/shard_map/psum | solution.py:362
  609.2 2.6 fusion.74
  611.8 27.2 %reduce-scatter.27.cloned.1.call-done = f32[96,192]{1,0:T(8,128)} async-done(((f32[768,192]{1,0:T(8,128)}), f32[96,192]{1,0:T(8,128)}) %reduce-scatter.27.cloned.1.call-update) | async-done | bytes 73744 | tf_op jit(solution)/shard_map/reduce_scatter | solution.py:368
  638.9 38.9 %reduce-scatter.25.cloned.1.call-done = f32[96,192]{1,0:T(8,128)} async-done(((f32[768,192]{1,0:T(8,128)}), f32[96,192]{1,0:T(8,128)}) %reduce-scatter.25.cloned.1.call-update) | async-done | bytes 73744 | tf_op jit(solution)/shard_map/reduce_scatter | solution.py:367
  677.8 39.0 %reduce-scatter.29.cloned.1.call-done = f32[96,192]{1,0:T(8,128)} async-done(((f32[768,192]{1,0:T(8,128)}), f32[96,192]{1,0:T(8,128)}) %reduce-scatter.29.cloned.1.call-update) | async-done | bytes 73744 | tf_op jit(solution)/shard_map/reduce_scatter | solution.py:369
  716.9 96.8 %reduce-scatter.35.cloned.1.call-done = f32[8,512,96]{1,2,0:T(8,128)} async-done(((f32[8,512,768]{1,2,0:T(8,128)}), f32[8,512,96]{1,2,0:T(8,128)}) %reduce-scatter.35.cloned.1.call-update) | async-done | bytes 1572880 | tf_op jit(solution)/shard_map/reduce_scatter | solution.py:373
  813.6 96.7 %reduce-scatter.31.cloned.1.call-done = f32[8,96,512]{2,1,0:T(8,128)} async-done(((f32[8,768,512]{2,1,0:T(8,128)}), f32[8,96,512]{2,1,0:T(8,128)}) %reduce-scatter.31.cloned.1.call-update) | async-done | bytes 1572880 | tf_op jit(solution)/shard_map/reduce_scatter | solution.py:371
  910.4 96.8 %reduce-scatter.33.cloned.1.call-done = f32[8,96,512]{2,1,0:T(8,128)} async-done(((f32[8,768,512]{2,1,0:T(8,128)}), f32[8,96,512]{2,1,0:T(8,128)}) %reduce-scatter.33.cloned.1.call-update) | async-done | bytes 1572880 | tf_op jit(solution)/shard_map/reduce_scatter | solution.py:372
  (417 shorter events, 70.4 us)
Async XLA Ops:
  7.2 67.7 %copy-start = (bf16[192,768]{1,0:T(8,128)(2,1)S(1)}, bf16[192,768]{1,0:T(8,128)(2,1)}, u32[]{:S(2)}) copy-start(bf16[192,768]{1,0:T(8,128)(2,1)} %param.25) | copy-start | bytes 884740
  7.2 46.4 %copy-start.48 = (bf16[768,192]{0,1:T(8,128)(2,1)S(1)}, bf16[768,192]{0,1:T(8,128)(2,1)}, u32[]{:S(2)}) copy-start(bf16[768,192]{0,1:T(8,128)(2,1)} %param.23) | copy-start | bytes 884740
  7.2 44.3 %all-gather.5.cloned.1.call-start = ((), (), s32[]{:S(2)}) async-start(), calls=%async_computation.12 | async-start | bytes 1966080 | tf_op jit(solution)/shard_map/all_gather | solution.py:207
  11.5 99.5 %reduce-scatter.17.cloned.1.call-start = ((), (), s32[]{:S(2)}) async-start(), calls=%async_computation.13 | async-start | bytes 1966080 | tf_op jit(solution)/shard_map/reduce_scatter | solution.py:223
  12.1 43.9 %copy-start.44 = (f32[1024,32]{0,1:T(8,128)}, f32[1024,32]{0,1:T(8,128)S(1)}, u32[]{:S(2)}) copy-start(f32[1024,32]{0,1:T(8,128)S(1)} %get-tuple-element.445) | copy-start | bytes 393220
  12.2 43.9 %copy-start.46 = (f32[1024,32]{0,1:T(8,128)}, f32[1024,32]{0,1:T(8,128)S(1)}, u32[]{:S(2)}) copy-start(f32[1024,32]{0,1:T(8,128)S(1)} %get-tuple-element.446) | copy-start | bytes 393220
  74.9 36.1 %copy-start.12 = (bf16[256,768]{1,0:T(8,128)(2,1)S(1)}, bf16[256,768]{1,0:T(8,128)(2,1)}, u32[]{:S(2)}) copy-start(bf16[256,768]{1,0:T(8,128)(2,1)} %param.20) | copy-start | bytes 1179652
  76.7 35.6 %copy-start.65 = (f32[768]{0:T(1024)S(1)}, f32[768]{0:T(1024)}, u32[]{:S(2)}) copy-start(f32[768]{0:T(1024)} %param.26) | copy-start | bytes 9220
  76.7 38.0 %copy-start.28 = (bf16[256,768]{1,0:T(8,128)(2,1)S(1)}, bf16[256,768]{1,0:T(8,128)(2,1)}, u32[]{:S(2)}) copy-start(bf16[256,768]{1,0:T(8,128)(2,1)} %param.35) | copy-start | bytes 1179652
  76.7 72.0 %all-gather.9.cloned.1.call-start = ((), (), s32[]{:S(2)}) async-start(), calls=%async_computation.16 | async-start | bytes 1966080 | tf_op jit(solution)/shard_map/all_gather | solution.py:283
  77.5 109.2 %all-gather.7.cloned.1.call-start = ((), (), s32[]{:S(2)}) async-start(), calls=%async_computation.14 | async-start | bytes 1966080 | tf_op jit(solution)/shard_map/all_gather | solution.py:229
  78.0 37.9 %copy-start.62 = (s32[2048]{0:T(1024)}, s32[2048]{0:T(1024)S(1)}, u32[]{:S(2)}) copy-start(s32[2048]{0:T(1024)S(1)} %eq.75) | copy-start | bytes 24580
  114.4 232.9 %reduce-scatter.37.cloned.1.call-start = ((), (), s32[]{:S(2)}) async-start(), calls=%async_computation.26 | async-start | bytes 327680
  119.0 41.4 %copy-start.82 = (s32[2048,1]{0,1:T(1,128)}, s32[2048,1]{0,1:T(1,128)S(1)}, u32[]{:S(2)}) copy-start(s32[2048,1]{0,1:T(1,128)S(1)} %compare_select_fusion) | copy-start | bytes 24580
  189.5 17.5 %copy-start.58 = (s32[1024,2]{0,1:T(2,128)S(1)}, s32[1024,2]{0,1:T(2,128)}, u32[]{:S(2)}) copy-start(s32[1024,2]{0,1:T(2,128)} %param.34) | copy-start | bytes 24580
  189.5 18.0 %copy-start.63 = (s32[2048]{0:T(1024)S(1)}, s32[2048]{0:T(1024)}, u32[]{:S(2)}) copy-start(s32[2048]{0:T(1024)} %copy-done.62) | copy-start | bytes 24580
  189.5 30.0 %copy-start.101 = (s32[1024]{0:T(1024)S(1)}, s32[1024]{0:T(1024)}, u32[]{:S(2)}) copy-start(s32[1024]{0:T(1024)} %get-tuple-element.369) | copy-start | bytes 12292
  189.6 30.0 %copy-start.102 = (s32[1024]{0:T(1024)S(1)}, s32[1024]{0:T(1024)}, u32[]{:S(2)}) copy-start(s32[1024]{0:T(1024)} %get-tuple-element.370) | copy-start | bytes 12292
  207.3 18.3 %slice-start.2 = ((s8[6291456]{0:T(1024)(128)(4,1)}), s8[2097152]{0:T(1024)(128)(4,1)S(1)}, s32[]{:S(2)}) async-start(s8[6291456]{0:T(1024)(128)(4,1)} %bitcast.212), calls=%async_computation.30 | async-start | bytes 4194304
  219.5 16.4 %copy-start.76 = (f32[8,256]{1,0:T(8,128)}, f32[8,256]{1,0:T(8,128)S(1)}, u32[]{:S(2)}) copy-start(f32[8,256]{1,0:T(8,128)S(1)} %mul.753) | copy-start | bytes 24580
  219.6 6.0 slice-start.3
  278.6 22.5 %slice-start.4 = ((s8[6291456]{0:T(1024)(128)(4,1)}), s8[2097152]{0:T(1024)(128)(4,1)S(1)}, s32[]{:S(2)}) async-start(s8[6291456]{0:T(1024)(128)(4,1)} %bitcast.214), calls=%async_computation.32 | async-start | bytes 4194304
  295.7 79.6 %reduce-scatter.21.cloned.1.call-start = ((), (), s32[]{:S(2)}) async-start(), calls=%async_computation.17 | async-start | bytes 1966080 | tf_op jit(solution)/shard_map/reduce_scatter | solution.py:320
  329.3 11.7 %copy-start.100 = (f32[256,2,2]{0,2,1:T(2,128)S(1)}, f32[256,2,2]{0,2,1:T(2,128)}, u32[]{:S(2)}) copy-start(f32[256,2,2]{0,2,1:T(2,128)} %fusion.78) | copy-start | bytes 12292
  329.3 11.9 %copy-start.99 = (f32[256,2]{0,1:T(2,128)S(1)}, f32[256,2]{0,1:T(2,128)}, u32[]{:S(2)}) copy-start(f32[256,2]{0,1:T(2,128)} %copy.147) | copy-start | bytes 6148
  329.3 11.9 %copy-start.19 = (f32[256,768]{1,0:T(8,128)S(1)}, f32[256,768]{1,0:T(8,128)}, u32[]{:S(2)}) copy-start(f32[256,768]{1,0:T(8,128)} %get-tuple-element.412) | copy-start | bytes 2359300
  329.3 11.9 %copy-start.87 = (f32[2,768]{1,0:T(2,128)S(1)}, f32[2,768]{1,0:T(2,128)}, u32[]{:S(2)}) copy-start(f32[2,768]{1,0:T(2,128)} %param.30) | copy-start | bytes 18436
  341.0 75.3 %all-gather.11.cloned.1.call-start = ((), (), s32[]{:S(2)}) async-start(), calls=%async_computation.18 | async-start | bytes 1966080 | tf_op jit(solution)/shard_map/all_gather | solution.py:330
  348.6 25.9 %copy-start.52 = (f32[256,12]{0,1:T(8,128)S(1)}, f32[256,12]{0,1:T(8,128)}, u32[]{:S(2)}) copy-start(f32[256,12]{0,1:T(8,128)} %copy-done.51) | copy-start | bytes 36868
  348.6 25.9 %copy-start.73 = (f32[256]{0:T(256)S(1)}, f32[256]{0:T(256)}, u32[]{:S(2)}) copy-start(f32[256]{0:T(256)} %copy-done.72) | copy-start | bytes 3076
  348.6 26.7 %copy-start.13 = (bf16[256,768]{1,0:T(8,128)(2,1)S(1)}, bf16[256,768]{1,0:T(8,128)(2,1)}, u32[]{:S(2)}) copy-start(bf16[256,768]{1,0:T(8,128)(2,1)} %param.20) | copy-start | bytes 1179652
  348.6 26.7 %copy-start.21 = (bf16[256,768]{1,0:T(8,128)(2,1)S(1)}, bf16[256,768]{1,0:T(8,128)(2,1)}, u32[]{:S(2)}) copy-start(bf16[256,768]{1,0:T(8,128)(2,1)} %reduce-scatter.17.cloned.1.call-done) | copy-start | bytes 1179652
  348.6 26.7 %copy-start.54 = (f32[768,12]{0,1:T(8,128)S(1)}, f32[768,12]{0,1:T(8,128)}, u32[]{:S(2)}) copy-start(f32[768,12]{0,1:T(8,128)} %param.27) | copy-start | bytes 110596
  348.6 26.7 %copy-start.66 = (f32[768]{0:T(1024)S(1)}, f32[768]{0:T(1024)}, u32[]{:S(2)}) copy-start(f32[768]{0:T(1024)} %param.26) | copy-start | bytes 9220
  348.6 26.7 %copy-start.84 = (f32[256]{0:T(256)S(1)}, f32[256]{0:T(256)}, u32[]{:S(2)}) copy-start(f32[256]{0:T(256)} %copy-done.83) | copy-start | bytes 3076
  348.6 29.5 %copy-start.95 = (f32[256]{0:T(256)S(1)}, f32[256]{0:T(256)}, u32[]{:S(2)}) copy-start(f32[256]{0:T(256)} %copy-done.94) | copy-start | bytes 3076
  374.5 5.7 copy-start.37
  379.0 39.4 %copy-start.24 = (bf16[1,1024,3,64]{1,3,2,0:T(8,128)(2,1)S(1)}, bf16[1,1024,3,64]{1,3,2,0:T(8,128)(2,1)}, u32[]{:S(2)}) copy-start(bf16[1,1024,3,64]{1,3,2,0:T(8,128)(2,1)} %copy-done.23) | copy-start | bytes 1179652
  379.0 39.4 %copy-start.60 = (f32[2,3,512]{2,1,0:T(4,128)S(1)}, f32[2,3,512]{2,1,0:T(4,128)}, u32[]{:S(2)}) copy-start(f32[2,3,512]{2,1,0:T(4,128)} %copy-done.59) | copy-start | bytes 36868
  380.1 152.6 %reduce-scatter.39.cloned.1.call-start = ((), (), s32[]{:S(2)}) async-start(), calls=%async_computation.27 | async-start | bytes 884736
  418.4 7.4 copy-start.34
  446.4 5.8 copy-start.7
  446.4 5.8 copy-start.16
  446.4 5.8 copy-start.25
  446.4 5.8 copy-start.35
  452.2 7.4 copy-start.34
  480.5 5.9 copy-start.7
  480.5 5.9 copy-start.16
  480.5 5.9 copy-start.25
  480.5 5.9 copy-start.35
  491.6 71.7 %reduce-scatter.23.cloned.1.call-start = ((), (), s32[]{:S(2)}) async-start(), calls=%async_computation.19 | async-start | bytes 1966080 | tf_op jit(solution)/shard_map/reduce_scatter | solution.py:357
  496.3 112.8 %reduce-scatter.19.cloned.1.call-start = ((), (), s32[]{:S(2)}) async-start(), calls=%async_computation.15 | async-start | bytes 1966080 | tf_op jit(solution)/shard_map/reduce_scatter | solution.py:267
  496.9 142.0 %reduce-scatter.27.cloned.1.call-start = ((), (), s32[]{:S(2)}) async-start(), calls=%async_computation.21 | async-start | bytes 884736 | tf_op jit(solution)/shard_map/reduce_scatter | solution.py:368
  499.3 178.5 %reduce-scatter.25.cloned.1.call-start = ((), (), s32[]{:S(2)}) async-start(), calls=%async_computation.20 | async-start | bytes 884736 | tf_op jit(solution)/shard_map/reduce_scatter | solution.py:367
  501.0 215.8 %reduce-scatter.29.cloned.1.call-start = ((), (), s32[]{:S(2)}) async-start(), calls=%async_computation.22 | async-start | bytes 884736 | tf_op jit(solution)/shard_map/reduce_scatter | solution.py:369
  502.6 311.0 %reduce-scatter.35.cloned.1.call-start = ((), (), s32[]{:S(2)}) async-start(), calls=%async_computation.25 | async-start | bytes 14155776 | tf_op jit(solution)/shard_map/reduce_scatter | solution.py:373
  512.4 397.9 %reduce-scatter.31.cloned.1.call-start = ((), (), s32[]{:S(2)}) async-start(), calls=%async_computation.23 | async-start | bytes 14155776 | tf_op jit(solution)/shard_map/reduce_scatter | solution.py:371
  522.3 484.8 %reduce-scatter.33.cloned.1.call-start = ((), (), s32[]{:S(2)}) async-start(), calls=%async_computation.24 | async-start | bytes 14155776 | tf_op jit(solution)/shard_map/reduce_scatter | solution.py:372
  530.4 32.9 %copy-start.14 = (bf16[256,768]{1,0:T(8,128)(2,1)S(1)}, bf16[256,768]{1,0:T(8,128)(2,1)}, u32[]{:S(2)}) copy-start(bf16[256,768]{1,0:T(8,128)(2,1)} %param.20) | copy-start | bytes 1179652
  530.4 32.9 %copy-start.71 = (f32[768]{0:T(1024)S(1)}, f32[768]{0:T(1024)}, u32[]{:S(2)}) copy-start(f32[768]{0:T(1024)} %param.21) | copy-start | bytes 9220
  530.4 78.7 %copy-start.22 = (bf16[256,768]{1,0:T(8,128)(2,1)S(1)}, bf16[256,768]{1,0:T(8,128)(2,1)}, u32[]{:S(2)}) copy-start(bf16[256,768]{1,0:T(8,128)(2,1)} %reduce-scatter.17.cloned.1.call-done) | copy-start | bytes 1179652
  530.4 78.7 %copy-start.27 = (f32[256,768]{1,0:T(8,128)S(1)}, f32[256,768]{1,0:T(8,128)}, u32[]{:S(2)}) copy-start(f32[256,768]{1,0:T(8,128)} %copy-done.26) | copy-start | bytes 2359300
  530.4 78.7 %copy-start.30 = (bf16[256,768]{1,0:T(8,128)(2,1)S(1)}, bf16[256,768]{1,0:T(8,128)(2,1)}, u32[]{:S(2)}) copy-start(bf16[256,768]{1,0:T(8,128)(2,1)} %param.35) | copy-start | bytes 1179652
  530.5 78.7 %copy-start.32 = (f32[256,768]{1,0:T(8,128)S(1)}, f32[256,768]{1,0:T(8,128)}, u32[]{:S(2)}) copy-start(f32[256,768]{1,0:T(8,128)} %get-tuple-element.357) | copy-start | bytes 2359300
  (72 other events, 211.2 us)
Sparse Core Ops, SparseCore 0:
  11.6 39.7 all-gather.4
  76.8 34.1 reduce-scatter.16
  112.6 36.1 all-gather.8
  150.7 35.9 all-gather.6
  295.8 18.5 reduce-scatter.36
  341.1 34.1 reduce-scatter.20
  380.2 36.0 all-gather.10
  491.7 33.8 reduce-scatter.38
  528.0 35.2 reduce-scatter.22
  565.6 35.3 reduce-scatter.18
  605.0 33.9 reduce-scatter.26
  642.8 34.9 reduce-scatter.24
  681.9 34.9 reduce-scatter.28
  721.2 92.3 reduce-scatter.34
  817.9 92.3 reduce-scatter.30
  914.7 92.3 reduce-scatter.32
where the time goes:
time: 1020 us; the launch traced here: 1010 us
  waiting for transfers between devices  560 us (55%)
  matrix products  143 us (14%)
  local copies, waits for them, and re-layouts  138 us (14%)
  other arithmetic  102 us (10%)
  blocking collectives  43.9 us (4%)
  between operations  15.9 us (2%)
    reduce_scatter x1, waiting for transfers between devices, on_device(): lax.psum_scatter(down_part, 'dp', scatter_dimension=2, tiled=True)  96.8 us
    reduce_scatter x1, waiting for transfers between devices, on_device(): lax.psum_scatter(up_part, 'dp', scatter_dimension=1, tiled=True)  96.8 us
    reduce_scatter x1, waiting for transfers between devices, on_device(): lax.psum_scatter(gate_part, 'dp', scatter_dimension=1, tiled=True)  96.7 us
    psum x1, blocking collectives, on_device(): lax.psum((attn_gain_part, moe_gain_part, router_part, const_gate_part, co...  43.9 us
    all_gather x1, waiting for transfers between devices, on_device(): attn_rows = lax.all_gather(norm_attn, 'tensor', axis=0, tiled=True)  39.3 us
    reduce_scatter x1, waiting for transfers between devices, on_device(): lax.psum_scatter(value_part, 'dp', scatter_dimension=0, tiled=True)  39 us
    reduce_scatter x1, waiting for transfers between devices, on_device(): lax.psum_scatter(query_part, 'dp', scatter_dimension=0, tiled=True)  38.9 us
    all_gather x1, waiting for transfers between devices, on_device(): lax.all_gather(hidden_grad.astype(jnp.bfloat16), 'tensor', axis=0, tiled=...  36 us
  transfers between devices with their start and end apart: 16, of which 13 were waited for; matrix products, arithmetic and copies ran while one was open for 17% of the time, Pallas kernels for 0%

commit v1 on v0

--- a/solution.py
+++ b/solution.py
@@ -1,8 +1,11 @@
+import functools
 import math
 
 import jax
 import jax.numpy as jnp
 from jax import lax
+from jax.experimental import pallas as pl
+from jax.experimental.pallas import tpu as pltpu
 from jax.sharding import PartitionSpec as P
 
 HD = 64
@@ -65,26 +68,228 @@
     return (key_pos // BLOCK)[None, :] <= (query_pos // BLOCK)[:, None]
 
 
-def side_experts(norm_values, router_w, mix_weight, const_rows, residual_logits, picks, ffn_count):
-    logits = jnp.dot(norm_values, router_w, precision=lax.Precision.HIGHEST) + residual_logits
-    soft_probs = jax.nn.softmax(logits, axis=-1)
-    chosen = jnp.take_along_axis(soft_probs, picks, axis=1)
-    mixing = jax.nn.softmax(
-        jnp.einsum("rd,cdj->rcj", norm_values, mix_weight, precision=lax.Precision.HIGHEST), axis=-1
-    )
-    constant = (
-        mixing[..., 0:1] * norm_values[:, None, :] + mixing[..., 1:2] * const_rows[None, :, :]
-    )
-    special = (picks == ffn_count + 1).astype(jnp.float32)[..., None] * norm_values[:, None, :]
-    special = (
-        special
-        + (picks == ffn_count + 2).astype(jnp.float32)[..., None] * constant[:, 0][:, None, :]
-    )
-    special = (
-        special
-        + (picks == ffn_count + 3).astype(jnp.float32)[..., None] * constant[:, 1][:, None, :]
-    )
-    return (chosen, jnp.sum(chosen[..., None] * special, axis=1))
+def pad_router(router_weight, const_gate):
+    gates = jnp.transpose(const_gate, (1, 0, 2)).reshape(const_gate.shape[1], -1)
+    return jnp.concatenate([router_weight, gates], axis=1)
+
+
+def side_experts(norm, named, weights, residual, const_value, ffn_count):
+    route_count = named.shape[1]
+    both = jnp.dot(norm, weights, precision=lax.Precision.HIGHEST)
+    logits = both[:, :route_count] + residual
+    probs = jax.nn.softmax(logits, axis=-1)
+    mix = both[:, route_count:].reshape(norm.shape[0], 2, 2)
+    share = jax.nn.sigmoid(mix[:, :, 0] - mix[:, :, 1])
+    chosen = probs * named
+    return probs, share, chosen
+
+
+def side_sum(norm, share, chosen, const_value, ffn_count):
+    c9 = chosen[:, ffn_count + 1 : ffn_count + 2]
+    c10 = chosen[:, ffn_count + 2 : ffn_count + 4]
+    keep = c9 + jnp.sum(c10 * share, axis=1, keepdims=True)
+    mixed = keep * norm
+    rest = c10 * (1.0 - share)
+    mixed = mixed + rest[:, 0:1] * const_value[0:1] + rest[:, 1:2] * const_value[1:2]
+    return mixed, keep, rest
+
+
+def side_backward(norm, named, weights, const_value, probs, share, chosen, keep, rest, chosen_back, grad, ffn_count):
+    self_dot = jnp.sum(grad * norm, axis=1, keepdims=True)
+    value_dot = jnp.concatenate(
+        [jnp.sum(grad * const_value[c : c + 1], axis=1, keepdims=True) for c in range(2)], axis=1
+    )
+    special = jnp.concatenate(
+        [
+            jnp.zeros_like(self_dot),
+            self_dot,
+            share * self_dot + (1.0 - share) * value_dot,
+        ],
+        axis=1,
+    )
+    d_probs = jnp.concatenate([chosen_back, special], axis=1) * named
+    d_logits = probs * (d_probs - jnp.sum(probs * d_probs, axis=1, keepdims=True))
+    c10 = chosen[:, ffn_count + 2 : ffn_count + 4]
+    d_share = share * (1.0 - share) * c10 * (self_dot - value_dot)
+    d_mix = jnp.stack([d_share, -d_share], axis=2).reshape(norm.shape[0], 4)
+    d_both = jnp.concatenate([d_logits, d_mix], axis=1)
+    back = (
+        lax.dot_general(
+            d_both, weights, (((1,), (1,)), ((), ())), precision=lax.Precision.HIGHEST
+        )
+        + keep * grad
+    )
+    weight_part = lax.dot_general(
+        norm, d_both, (((0,), (0,)), ((), ())), precision=lax.Precision.HIGHEST
+    )
+    value_part = lax.dot_general(
+        rest, grad, (((0,), (0,)), ((), ())), precision=lax.Precision.HIGHEST
+    )
+    return back, weight_part, value_part
+
+
+EXP_PAD = 16
+
+
+def dot(a, b):
+    return jnp.dot(a, b, preferred_element_type=jnp.float32)
+
+
+def dot_nt(a, b):
+    return lax.dot_general(a, b, (((1,), (1,)), ((), ())), preferred_element_type=jnp.float32)
+
+
+def dot_tn(a, b):
+    return lax.dot_general(a, b, (((0,), (0,)), ((), ())), preferred_element_type=jnp.float32)
+
+
+def three_parts(values):
+    first = values.astype(jnp.bfloat16)
+    rest = values - first.astype(jnp.float32)
+    second = rest.astype(jnp.bfloat16)
+    third = (rest - second.astype(jnp.float32)).astype(jnp.bfloat16)
+    return (first, second, third)
+
+
+def expert_kernel(
+    n_dp,
+    ffn_count,
+    route_count,
+    moe_ref,
+    grad_ref,
+    routes_ref,
+    residual_ref,
+    router_ref,
+    gate_ref,
+    up_ref,
+    down_ref,
+    part_ref,
+    back_ref,
+    chosen_ref,
+    weight_ref,
+    probs_s,
+    rank_s,
+    part_s,
+    back_s,
+):
+    expert = pl.program_id(0)
+    rows = moe_ref.shape[0]
+    hidden = gate_ref.shape[2]
+    step = moe_ref.shape[1] // n_dp
+
+    @pl.when(expert == 0)
+    def _():
+        parts = three_parts(router_ref[...])
+        logits = residual_ref[...]
+        for part in parts:
+            logits = logits + dot_nt(part, moe_ref[...])
+        index = lax.broadcasted_iota(jnp.int32, (EXP_PAD, rows), 0)
+        logits = jnp.where(index < route_count, logits, MASKED)
+        top = jnp.max(logits, axis=0, keepdims=True)
+        exps = jnp.exp(logits - top)
+        probs_s[...] = exps / jnp.sum(exps, axis=0, keepdims=True)
+        named = (routes_ref[0:1, :] == index) | (routes_ref[1:2, :] == index)
+        named = jnp.where(named, 1.0, 0.0)
+        width = 256
+        before = lax.broadcasted_iota(jnp.int32, (width, width), 0)
+        after = lax.broadcasted_iota(jnp.int32, (width, width), 1)
+        earlier = jnp.where(before < after, 1.0, 0.0).astype(jnp.bfloat16)
+        total = jnp.zeros((EXP_PAD, 1), jnp.float32)
+        for start in range(0, rows, width):
+            block = named[:, start : start + width]
+            rank = dot(block.astype(jnp.bfloat16), earlier) + total
+            rank_s[:, start : start + width] = jnp.where(block > 0.5, rank, -1.0)
+            total = total + jnp.sum(block, axis=1, keepdims=True)
+        part_s[...] = jnp.zeros_like(part_s)
+        back_s[...] = jnp.zeros_like(back_s)
+
+    slot = lax.broadcasted_iota(jnp.int32, (CAP, rows), 0).astype(jnp.float32)
+    hit = rank_s[pl.ds(expert, 1), :] == slot
+    dispatch = jnp.where(hit, 1.0, 0.0).astype(jnp.bfloat16)
+    slot_weight = jnp.sum(
+        jnp.where(hit, probs_s[pl.ds(expert, 1), :], 0.0), axis=1, keepdims=True
+    )
+    rows_in = dot(dispatch, moe_ref[...]).astype(jnp.bfloat16)
+    rows_grad = dot(dispatch, grad_ref[...])
+    gate_w = gate_ref[0]
+    up_w = up_ref[0]
+    down_w = down_ref[0]
+    gate_pre = dot(rows_in, gate_w)
+    up_pre = dot(rows_in, up_w)
+    sigmoid = 1.0 / (1.0 + jnp.exp(-gate_pre))
+    silu = gate_pre * sigmoid
+    active = (silu * up_pre).astype(jnp.bfloat16)
+    out = dot(active, down_w)
+    inner = jnp.sum(rows_grad * out, axis=1, keepdims=True)
+    chosen_ref[pl.ds(expert, 1), :] = jnp.sum(jnp.where(hit, inner, 0.0), axis=0, keepdims=True)
+    part_s[...] += dot_tn(dispatch, (out * slot_weight).astype(jnp.bfloat16))
+    grad_low = (rows_grad * slot_weight).astype(jnp.bfloat16)
+    grad_active = dot_nt(grad_low, down_w)
+    grad_gate = (grad_active * up_pre * sigmoid * (1.0 + gate_pre * (1.0 - sigmoid))).astype(
+        jnp.bfloat16
+    )
+    grad_up = (grad_active * silu).astype(jnp.bfloat16)
+    grad_in = dot_nt(grad_gate, gate_w) + dot_nt(grad_up, up_w)
+    back_s[...] += dot_tn(dispatch, grad_in.astype(jnp.bfloat16))
+    for n, (left, right) in enumerate(
+        ((rows_in, grad_gate), (rows_in, grad_up), (grad_low, active))
+    ):
+        product = dot_tn(left, right).astype(jnp.bfloat16)
+        for d in range(n_dp):
+            weight_ref[0, d % 2, d // 2, :, n * hidden : (n + 1) * hidden] = product[
+                d * step : (d + 1) * step
+            ]
+
+    @pl.when(expert == ffn_count - 1)
+    def _():
+        part_ref[...] = part_s[...].astype(jnp.bfloat16)
+        back_ref[...] = back_s[...].astype(jnp.bfloat16)
+
+
+def experts(n_dp, route_count, moe_rows, grad_rows, routes_t, residual_t, router_t, gate_w, up_w, down_w):
+    rows, width = moe_rows.shape
+    ffn_count, _, hidden = gate_w.shape
+    step = width // n_dp
+
+    def whole(shape):
+        return pl.BlockSpec(shape, lambda e: (0,) * len(shape), pipeline_mode=pl.Buffered(1))
+
+    return pl.pallas_call(
+        functools.partial(expert_kernel, n_dp, ffn_count, route_count),
+        grid=(ffn_count,),
+        out_shape=(
+            jax.ShapeDtypeStruct((rows, width), jnp.bfloat16),
+            jax.ShapeDtypeStruct((rows, width), jnp.bfloat16),
+            jax.ShapeDtypeStruct((ffn_count, rows), jnp.float32),
+            jax.ShapeDtypeStruct((ffn_count, 2, n_dp // 2, step, 3 * hidden), jnp.bfloat16),
+        ),
+        in_specs=[
+            whole((rows, width)),
+            whole((rows, width)),
+            whole((2, rows)),
+            whole((EXP_PAD, rows)),
+            whole((EXP_PAD, width)),
+            pl.BlockSpec((1, width, hidden), lambda e: (e, 0, 0)),
+            pl.BlockSpec((1, width, hidden), lambda e: (e, 0, 0)),
+            pl.BlockSpec((1, hidden, width), lambda e: (e, 0, 0)),
+        ],
+        out_specs=(
+            whole((rows, width)),
+            whole((rows, width)),
+            whole((ffn_count, rows)),
+            pl.BlockSpec((1, 2, n_dp // 2, step, 3 * hidden), lambda e: (e, 0, 0, 0, 0)),
+        ),
+        scratch_shapes=[
+            pltpu.VMEM((EXP_PAD, rows), jnp.float32),
+            pltpu.VMEM((EXP_PAD, rows), jnp.float32),
+            pltpu.VMEM((rows, width), jnp.float32),
+            pltpu.VMEM((rows, width), jnp.float32),
+        ],
+        compiler_params=pltpu.CompilerParams(
+            dimension_semantics=("arbitrary",), vmem_limit_bytes=48 << 20
+        ),
+        name="experts",
+    )(moe_rows, grad_rows, routes_t, residual_t, router_t, gate_w, up_w, down_w)
 
 
 def attention_forward(query, key, value):
@@ -199,7 +404,6 @@
     head_count = query_weight.shape[1] // HD
     ffn_count = gate_weight.shape[0]
     route_count = router_weight.shape[1]
-    slot_count = ffn_count * CAP
     cosine, sine = rope_tables(LENGTH, HD)
     input_wide = layer_input.astype(jnp.float32)
     norm_attn, pull_attn_norm = jax.vjp(rms_norm, input_wide, attn_gain)
@@ -227,104 +431,46 @@
     norm_moe, pull_moe_norm = jax.vjp(rms_norm, hidden, moe_gain)
     norm_moe = norm_moe.astype(jnp.bfloat16)
     moe_rows = lax.all_gather(norm_moe, "tensor", axis=0, tiled=True)
-    logits = (
-        jnp.dot(moe_rows.astype(jnp.float32), router_weight, precision=lax.Precision.HIGHEST)
-        + gate_residual
-    )
-    chosen = jnp.take_along_axis(jax.nn.softmax(logits, axis=-1), routes, axis=1)
-    flat_routes = routes.reshape(-1)
-    onehot = (flat_routes[:, None] == jnp.arange(route_count, dtype=jnp.int32)[None, :]).astype(
-        jnp.int32
-    )
-    earlier = jnp.cumsum(onehot, axis=0) - onehot
-    slot_rank = jnp.sum(onehot * earlier, axis=1)
-    is_ffn = flat_routes < ffn_count
-    slot_index = jnp.where(is_ffn, flat_routes * CAP + slot_rank, slot_count)
-    pair_slot = slot_index.reshape(group_rows, 2)
-    slot_ids = jnp.arange(slot_count, dtype=jnp.int32)[:, None]
-    dispatch = (
-        (pair_slot[:, 0][None, :] == slot_ids) | (pair_slot[:, 1][None, :] == slot_ids)
-    ).astype(jnp.bfloat16)
-    expert_in = (
-        jnp.dot(dispatch, moe_rows, preferred_element_type=jnp.float32)
-        .astype(jnp.bfloat16)
-        .reshape(ffn_count, CAP, model_width)
-    )
-    gate_pre = jnp.einsum(
-        "ecd,edf->ecf", expert_in, gate_weight, preferred_element_type=jnp.float32
-    )
-    up_pre = jnp.einsum("ecd,edf->ecf", expert_in, up_weight, preferred_element_type=jnp.float32)
-    active = (jax.nn.silu(gate_pre) * up_pre).astype(jnp.bfloat16)
-    expert_part = jnp.einsum(
-        "ecf,efd->ecd", active, down_weight, preferred_element_type=jnp.float32
-    )
-    padded = jnp.concatenate(
-        [expert_part.reshape(slot_count, model_width), jnp.zeros((1, model_width), jnp.float32)],
-        axis=0,
-    )
-    picked = padded[slot_index].reshape(group_rows, 2, model_width)
-    ffn_part = jnp.sum(chosen[..., None] * picked, axis=1)
-    ffn_sum = lax.psum_scatter(
-        ffn_part.astype(jnp.bfloat16), "tensor", scatter_dimension=0, tiled=True
-    ).astype(jnp.float32)
+    both_weight = pad_router(router_weight, const_gate)
+    n_dp = lax.axis_size("dp")
+    grad_rows = lax.all_gather(grad_out, "tensor", axis=0, tiled=True)
+    pad = ((0, EXP_PAD - route_count), (0, 0))
+    ffn_part, ffn_back, chosen_t, expert_part = experts(
+        n_dp,
+        route_count,
+        moe_rows,
+        grad_rows,
+        routes.T,
+        jnp.pad(gate_residual.T, pad),
+        jnp.pad(router_weight.T, pad),
+        gate_weight,
+        up_weight,
+        down_weight,
+    )
+    ffn_sum = lax.psum_scatter(ffn_part, "tensor", scatter_dimension=0, tiled=True).astype(
+        jnp.float32
+    )
+    moe_back = lax.psum_scatter(ffn_back, "tensor", scatter_dimension=0, tiled=True).astype(
+        jnp.float32
+    )
+    chosen_back = lax.psum_scatter(chosen_t.T, "tensor", scatter_dimension=0, tiled=True)
     local_routes = lax.dynamic_slice_in_dim(routes, row_start, local_rows, 0)
     local_logits = lax.dynamic_slice_in_dim(gate_residual, row_start, local_rows, 0)
-
-    def side_local(norm_values, router_w, mix_weight, const_rows):
-        return side_experts(
-            norm_values, router_w, mix_weight, const_rows, local_logits, local_routes, ffn_count
-        )
-
-    (local_chosen, special_sum), pull_side = jax.vjp(
-        side_local, norm_moe.astype(jnp.float32), router_weight, const_gate, const_value
-    )
+    kinds = jnp.arange(route_count, dtype=jnp.int32)[None, :]
+    named = ((local_routes[:, 0:1] == kinds) | (local_routes[:, 1:2] == kinds)).astype(jnp.float32)
+    norm_wide = norm_moe.astype(jnp.float32)
+    probs, share, chosen = side_experts(
+        norm_wide, named, both_weight, local_logits, const_value, ffn_count
+    )
+    special_sum, keep, rest = side_sum(norm_wide, share, chosen, const_value, ffn_count)
     output = (hidden + ffn_sum + special_sum).astype(jnp.bfloat16)
     grad_wide = grad_out.astype(jnp.float32)
-    grad_rows = lax.all_gather(grad_out, "tensor", axis=0, tiled=True)
-    owner_index = (
-        jnp.zeros((slot_count + 1,), jnp.int32)
-        .at[slot_index]
-        .set(jnp.repeat(jnp.arange(group_rows, dtype=jnp.int32), 2))
-    )
-    slot_weight = (
-        jnp.zeros((slot_count + 1,), jnp.float32)
-        .at[slot_index]
-        .add(jnp.where(is_ffn, chosen.reshape(-1), 0.0))
-    )
-    grad_expert = (
-        (grad_rows[owner_index[:slot_count]].astype(jnp.float32) * slot_weight[:slot_count, None])
-        .astype(jnp.bfloat16)
-        .reshape(ffn_count, CAP, model_width)
-    )
-    chosen_part = jnp.sum(grad_rows.astype(jnp.float32)[:, None, :] * picked, axis=-1)
-    grad_active = jnp.einsum(
-        "ecd,efd->ecf", grad_expert, down_weight, preferred_element_type=jnp.float32
-    )
-    sigmoid_gate = jax.nn.sigmoid(gate_pre)
-    grad_gate = (
-        grad_active * up_pre * sigmoid_gate * (1.0 + gate_pre * (1.0 - sigmoid_gate))
-    ).astype(jnp.bfloat16)
-    grad_up = (grad_active * gate_pre * sigmoid_gate).astype(jnp.bfloat16)
-    grad_in_expert = jnp.einsum(
-        "ecf,edf->ecd", grad_gate, gate_weight, preferred_element_type=jnp.float32
-    ) + jnp.einsum("ecf,edf->ecd", grad_up, up_weight, preferred_element_type=jnp.float32)
-    down_part = jnp.einsum("ecf,ecd->efd", active, grad_expert, preferred_element_type=jnp.float32)
-    gate_part = jnp.einsum("ecd,ecf->edf", expert_in, grad_gate, preferred_element_type=jnp.float32)
-    up_part = jnp.einsum("ecd,ecf->edf", expert_in, grad_up, preferred_element_type=jnp.float32)
-    padded_grad = jnp.concatenate(
-        [grad_in_expert.reshape(slot_count, model_width), jnp.zeros((1, model_width), jnp.float32)],
-        axis=0,
-    )
-    ffn_back = jnp.sum(padded_grad[slot_index].reshape(group_rows, 2, model_width), axis=1)
-    moe_back, chosen_back = (
-        lax.psum_scatter(
-            ffn_back.astype(jnp.bfloat16), "tensor", scatter_dimension=0, tiled=True
-        ).astype(jnp.float32),
-        lax.psum_scatter(
-            chosen_part.astype(jnp.bfloat16), "tensor", scatter_dimension=0, tiled=True
-        ).astype(jnp.float32),
-    )
-    side_back, router_part, const_gate_part, const_value_part = pull_side((chosen_back, grad_wide))
+    side_back, both_part, const_value_part = side_backward(
+        norm_wide, named, both_weight, const_value, probs, share, chosen, keep, rest,
+        chosen_back, grad_wide, ffn_count,
+    )
+    router_part = both_part[:, :route_count]
+    const_gate_part = jnp.transpose(both_part[:, route_count:].reshape(model_width, 2, 2), (1, 0, 2))
     hidden_norm_back, moe_gain_part = pull_moe_norm(moe_back + side_back)
     hidden_grad = grad_wide + hidden_norm_back
     attn_grad_rows = lax.all_gather(hidden_grad.astype(jnp.bfloat16), "tensor", axis=0, tiled=True)
@@ -363,14 +509,28 @@
         (attn_gain_part, moe_gain_part, router_part, const_gate_part, const_value_part),
         ("dp", "tensor"),
     )
+    attn_parts = jnp.stack(
+        [query_part, key_part, value_part, out_part.T], axis=1
+    ).reshape(model_width, -1).astype(jnp.bfloat16)
+    attn_sums = lax.psum_scatter(attn_parts, "dp", scatter_dimension=0, tiled=True).astype(
+        jnp.float32
+    ).reshape(model_width // n_dp, 4, -1)
+    hidden_units = gate_weight.shape[2]
+    expert_part = jnp.transpose(expert_part, (2, 1, 3, 0, 4)).reshape(
+        model_width, -1
+    )
+    expert_sums = lax.psum_scatter(expert_part, "dp", scatter_dimension=0, tiled=True).astype(
+        jnp.float32
+    ).reshape(model_width // n_dp, ffn_count, 3 * hidden_units)
+    expert_sums = jnp.transpose(expert_sums, (1, 0, 2))
     weight_sums = (
-        lax.psum_scatter(query_part, "dp", scatter_dimension=0, tiled=True),
-        lax.psum_scatter(key_part, "dp", scatter_dimension=0, tiled=True),
-        lax.psum_scatter(value_part, "dp", scatter_dimension=0, tiled=True),
-        lax.psum_scatter(out_part, "dp", scatter_dimension=1, tiled=True),
-        lax.psum_scatter(gate_part, "dp", scatter_dimension=1, tiled=True),
-        lax.psum_scatter(up_part, "dp", scatter_dimension=1, tiled=True),
-        lax.psum_scatter(down_part, "dp", scatter_dimension=2, tiled=True),
+        attn_sums[:, 0],
+        attn_sums[:, 1],
+        attn_sums[:, 2],
+        attn_sums[:, 3].T,
+        expert_sums[:, :, :hidden_units],
+        expert_sums[:, :, hidden_units : 2 * hidden_units],
+        jnp.transpose(expert_sums[:, :, 2 * hidden_units :], (0, 2, 1)),
     )
     return (
         output,

time: 1020 us -> 651 us (0.64)
  waiting for transfers between devices: 560 us -> 386 us
  matrix products: 143 us -> 49.3 us
  other arithmetic: 102 us -> 27 us
  local copies, waits for them, and re-layouts: 138 us -> 70.2 us
  Pallas kernels: 0 us -> 42.2 us
    reduce_scatter x8 -> x5, waiting for transfers between devices: 396 us -> 171 us  [the longest x1 119 us: on_device(): lax.psum_scatter(expert_part, 'dp', scatter_dimension=0, tiled=True)]
    dot_general x17 -> x5, matrix products: 77.9 us -> 3.59 us  [the longest x1 2.17 us: side_backward(): lax.dot_general(d_both, weights, (((1,), (1,)), ((), ())), precision=lax....]
    gather x15 -> x0, local copies, waits for them, and re-layouts: 63.1 us -> none  [the longest x5 17.9 us: on_device(): jnp.take_along_axis(jax.nn.softmax(logits, axis=-1), routes, axis=1)]
    pallas_call x0 -> x1, Pallas kernels: none -> 42.2 us  [experts(): pl.pallas_call(functools.partial(expert_kernel, n_dp, ffn_count, route_co...]
    scatter-add x2 -> x0, other arithmetic: 37.7 us -> none  [the longest x1 25.8 us: side_experts(): chosen = jnp.take_along_axis(soft_probs, picks, axis=1)]
    reduce_sum x9 -> x3, other arithmetic: 32.9 us -> 2.9 us  [the longest x1 2.09 us: side_backward(): jnp.sum(grad * const_value[c:c + 1], axis=1, keepdims=True)]
    all_gather x1, waiting for transfers between devices: 10.8 us -> 38 us  [on_device(): moe_rows = lax.all_gather(norm_moe, 'tensor', axis=0, tiled=True)]
    transpose x0 -> x3, local copies, waits for them, and re-layouts: none -> 19.3 us  [the longest x1 17.9 us: on_device(): jnp.transpose(expert_part, (2, 1, 3, 0, 4)).reshape(model_width, -1)]
  transfers between devices with their start and end apart: 16 -> 11, of which waited for: 13 -> 10; matrix products, arithmetic and copies ran while one was open for 17% -> 8% of each run, Pallas kernels for 0% -> 0%
where the time goes in v1:
time: 651 us; the launch traced here: 644 us
  waiting for transfers between devices  386 us (59%)
  local copies, waits for them, and re-layouts  70.2 us (11%)
  matrix products  49.3 us (8%)
  blocking collectives  43.4 us (7%)
  Pallas kernels  42.2 us (6%)
  other arithmetic  27 us (4%)
  between operations  14.9 us (2%)
  loops' own time  9.31 us (1%)
    reduce_scatter x1, waiting for transfers between devices, on_device(): lax.psum_scatter(expert_part, 'dp', scatter_dimension=0, tiled=True)  119 us
    psum x1, blocking collectives, on_device(): lax.psum((attn_gain_part, moe_gain_part, router_part, const_gate_part, co...  43.4 us
    pallas_call x1, Pallas kernels, experts(): pl.pallas_call(functools.partial(expert_kernel, n_dp, ffn_count, route_co...  42.2 us
    all_gather x1, waiting for transfers between devices, on_device(): attn_rows = lax.all_gather(norm_attn, 'tensor', axis=0, tiled=True)  39.3 us
    all_gather x1, waiting for transfers between devices, on_device(): moe_rows = lax.all_gather(norm_moe, 'tensor', axis=0, tiled=True)  38 us
    all_gather x1, waiting for transfers between devices, on_device(): lax.all_gather(hidden_grad.astype(jnp.bfloat16), 'tensor', axis=0, tiled=...  34.9 us
    reduce_scatter x1, waiting for transfers between devices, on_device(): lax.psum_scatter(ffn_back, 'tensor', scatter_dimension=0, tiled=True)  34.7 us
    reduce_scatter x1, waiting for transfers between devices, on_device(): lax.psum_scatter(attn_back.astype(jnp.bfloat16), 'tensor', scatter_dimens...  34 us
  transfers between devices with their start and end apart: 11, of which 10 were waited for; matrix products, arithmetic and copies ran while one was open for 8% of the time, Pallas kernels for 0%

profile of v1, /device:TPU:0, one launch (start us, length us, event | category | flops | bytes accessed | tf_op | source)
XLA Modules:
  0.0 643.6 jit_solution(7160567234504975469)
XLA Ops:
  7.3 1.2 fusion.65
  8.5 1.9 fusion.57
  11.1 39.3 %all-gather.5.cloned.1.call-done = bf16[1024,768]{1,0:T(8,128)(2,1)} async-done(((bf16[256,768]{1,0:T(8,128)(2,1)}), bf16[1024,768]{1,0:T(8,128)(2,1)}) %all-gather.5.cloned.1.call-update) | async-done | bytes 1572880 | tf_op jit(solution)/shard_map/all_gather | solution.py:411
  50.4 2.1 fusion.99
  52.5 2.2 fusion.98
  55.1 1.4 convolution_convert_fusion.2
  56.5 18.8 %while.44 = (s32[]{:T(128)}, bf16[2,512,3,64]{1,3,2,0:T(8,128)(2,1)S(1)}, f32[2,3,512]{2,1,0:T(4,128)S(1)}, s32[2]{0:T(128)S(1)}, bf16[1,1024,3,64]{1,3,2,0:T(8,...) while((s32[]{:T(128)}, ...), condition=%wide.region_4.5_spmd, body=%wide.region_1.4_spmd.sunk | while | flops 422066688 | bytes 22419764 | solution.py:322
  59.4 1.4 fusion.154
  60.8 1.8 fusion.155
  62.6 3.2 fusion.156
  68.8 1.4 fusion.154
  70.2 1.8 fusion.155
  72.0 3.2 fusion.156
  75.8 1.8 convolution_convert_fusion
  78.5 33.5 %reduce-scatter.8.cloned.1.call-done = bf16[256,768]{1,0:T(8,128)(2,1)} async-done(((bf16[1024,768]{1,0:T(8,128)(2,1)}), bf16[256,768]{1,0:T(8,128)(2,1)}) %reduce-scatter.8.cloned.1.call-update) | async-done | bytes 393232 | tf_op jit(solution)/shard_map/reduce_scatter | solution.py:427
  112.0 1.2 multiply_reduce_fusion.3
  113.2 2.1 fusion.68
  115.9 33.7 %all-gather.9.cloned.1.call-done.grad_ref = bf16[1024,768]{1,0:T(8,128)(2,1)} async-done(((bf16[256,768]{1,0:T(8,128)(2,1)}), bf16[1024,768]{1,0:T(8,128)(2,1)}) %all-gather.9.cloned.1.call-update) | async-done | bytes 1572880 | tf_op jit(solution)/shard_map/all_gather | solution.py:436
  149.6 38.0 %all-gather.7.cloned.1.call-done.moe_ref = bf16[1024,768]{1,0:T(8,128)(2,1)} async-done(((bf16[256,768]{1,0:T(8,128)(2,1)}), bf16[1024,768]{1,0:T(8,128)(2,1)}) %all-gather.7.cloned.1.call-update) | async-done | bytes 1572880 | tf_op jit(solution)/shard_map/all_gather | solution.py:433
  187.6 1.4 copy-done.2
  189.0 42.2 %experts.1 = (bf16[1024,768]{1,0:T(8,128)(2,1)}, bf16[1024,768]{1,0:T(8,128)(2,1)}, f32[8,1024]{1,0:T(8,128)}, bf16[8,2,4,96,1536]{4,3,2,1,0:T(8,128)(2,1)}) custom-call(bf16[1024,768]{1,0:T(8,128)(2,1)S(1)} %copy-done.2, bf16[1024,768]{1,0:T(8,128)(2,1)} %all-gather.9.cloned.1.call-done.grad_ref, s32[2,1024]{1,0:T(2,128)S(1)} %bitcast.194, ...), custom_call_target="tpu_custom_call" | custom-call | tf_op jit(solution)/shard_map/experts/pallas_call | solution.py:257
  232.7 16.5 %reduce-scatter.14.cloned.1.call-done = f32[256,8]{0,1:T(8,128)} async-done(((f32[1024,8]{0,1:T(8,128)}), f32[256,8]{0,1:T(8,128)}) %reduce-scatter.14.cloned.1.call-update) | async-done | bytes 8208 | tf_op jit(solution)/shard_map/reduce_scatter | solution.py:456
  249.2 0.8 multiply_reduce_fusion.4
  250.0 0.8 subtract_multiply_fusion
  250.8 34.7 %reduce-scatter.12.cloned.1.call-done = bf16[256,768]{1,0:T(8,128)(2,1)} async-done(((bf16[1024,768]{1,0:T(8,128)(2,1)}), bf16[256,768]{1,0:T(8,128)(2,1)}) %reduce-scatter.12.cloned.1.call-update) | async-done | bytes 393232 | tf_op jit(solution)/shard_map/reduce_scatter | solution.py:453
  285.5 2.2 multiply_reduce_fusion.1
  287.7 0.9 copy-done.14
  288.6 1.0 fusion.91
  289.9 1.1 pad_maximum_fusion.3
  291.0 34.9 %all-gather.11.cloned.1.call-done = bf16[1024,768]{1,0:T(8,128)(2,1)} async-done(((bf16[256,768]{1,0:T(8,128)(2,1)}), bf16[1024,768]{1,0:T(8,128)(2,1)}) %all-gather.11.cloned.1.call-update) | async-done | bytes 1572880 | tf_op jit(solution)/shard_map/all_gather | solution.py:476
  325.9 2.8 convolution_convert_fusion.1
  328.7 48.6 %while.45 = (s32[]{:T(128)}, f32[1024,3,64]{0,2,1:T(8,128)S(1)}, f32[1024,3,64]{0,2,1:T(8,128)}, f32[2,512,3,64]{1,0,3,2:T(2,128)}, s32[2]{0:T(128)S(1)}, /*inde...) while((s32[]{:T(128)}, f32[1024,3,64]{0,2,1:T(8,128)S(1)}, ...), condition=%wide.region_20.21_spmd.clone, body=%wide.region_18.20_spmd.clone.sunk | while | flops 1031846400 | bytes 56416532 | solution.py:373
  332.3 1.0 fusion.166
  333.4 3.8 fusion.168
  337.1 3.6 multiply_reduce_fusion.6
  340.7 1.8 multiply_convert_fusion.4
  342.5 1.1 fusion.169
  343.6 0.8 fusion.167
  344.8 8.1 %dynamic_update_slice.38 = f32[2,512,3,64]{1,0,3,2:T(2,128)} dynamic-update-slice(f32[2,512,3,64]{1,0,3,2:T(2,128)} %get-tuple-element.653, f32[1,512,3,64]{1,0,3,2:T(1,128)S(1)} %copy.99, s32[]{:T(128)S(6)} %copy.116, s32[]{:T(128)} %constant.272.clone.1..sunk.1, s32[]{:T(128)} %constant.272.clone.1..sunk.1, s32[]{:T(128)} %constant.272.clone.1..sunk.1) | dynamic-update-slice | bytes 786436 | tf_op jit(solution)/shard_map/while/body/eval_jaxpr/while/body/jit(dynamic_update_index_in_dim)/dynamic_update_slice | solution.py:322
  356.5 1.0 fusion.166
  357.5 4.1 fusion.168
  361.6 3.6 multiply_reduce_fusion.6
  365.2 1.8 multiply_convert_fusion.4
  367.0 1.1 fusion.169
  368.1 0.8 fusion.167
  369.3 8.1 %dynamic_update_slice.38 = f32[2,512,3,64]{1,0,3,2:T(2,128)} dynamic-update-slice(f32[2,512,3,64]{1,0,3,2:T(2,128)} %get-tuple-element.653, f32[1,512,3,64]{1,0,3,2:T(1,128)S(1)} %copy.99, s32[]{:T(128)S(6)} %copy.116, s32[]{:T(128)} %constant.272.clone.1..sunk.1, s32[]{:T(128)} %constant.272.clone.1..sunk.1, s32[]{:T(128)} %constant.272.clone.1..sunk.1) | dynamic-update-slice | bytes 786436 | tf_op jit(solution)/shard_map/while/body/eval_jaxpr/while/body/jit(dynamic_update_index_in_dim)/dynamic_update_slice | solution.py:322
  377.3 2.7 broadcast_in_dim.117
  380.1 1.3 convert_element_type.158
  381.4 1.5 add_convert_fusion.1
  385.1 1.5 copy.46
  386.9 1.6 fusion.100
  389.2 1.8 add_convert_fusion
  391.6 17.9 %copy.47 = bf16[4,2,96,8,1536]{4,3,2,1,0:T(8,128)(2,1)S(1)} copy(bf16[4,2,96,8,1536]{4,2,0,1,3:T(8,128)(2,1)} %bitcast.198) | data formatting | bytes 37748736 | tf_op jit(solution)/shard_map/transpose | solution.py:519
  409.5 12.0 %copy.76 = bf16[96,8,8,1536]{3,1,2,0:T(8,128)(2,1)} copy(bf16[96,8,8,1536]{3,2,1,0:T(8,128)(2,1)S(1)} %bitcast.196) | data formatting | bytes 37748736
  422.4 1.2 reshape.449
  426.6 34.0 %reduce-scatter.16.cloned.1.call-done = bf16[256,768]{1,0:T(8,128)(2,1)} async-done(((bf16[1024,768]{1,0:T(8,128)(2,1)}), bf16[256,768]{1,0:T(8,128)(2,1)}) %reduce-scatter.16.cloned.1.call-update) | async-done | bytes 393232 | tf_op jit(solution)/shard_map/reduce_scatter | solution.py:503
  460.6 1.3 fusion.62
  462.0 43.4 %all-reduce.2 = (f32[768]{0:T(1024)}, f32[768]{0:T(1024)}, f32[768,12]{0,1:T(8,128)}, f32[2,768,2]{1,2,0:T(2,128)}, f32[2,768]{1,0:T(2,128)}) all-reduce(f32[768]{0:T(1024)S(1)} %get-tuple-element.392, f32[768]{0:T(1024)S(1)} %get-tuple-element.390, f32[768,12]{0,1:T(8,128)S(1)} %bitcast.217, ...), channel_id=1, replica_groups=mesh['dp'=8,'tensor'=4] {'dp','tensor'}, use_global_device_ids=true, to_apply=%region_24.25 | all-reduce | flops 15360 | bytes 122880 | tf_op jit(solution)/shard_map/psum | solution.py:508
  505.5 2.8 fusion.64
  508.2 119.2 %reduce-scatter.20.cloned.1.call-done = bf16[96,12288]{1,0:T(8,128)(2,1)} async-done(((bf16[768,12288]{1,0:T(8,128)(2,1)}), bf16[96,12288]{1,0:T(8,128)(2,1)}) %reduce-scatter.20.cloned.1.call-update) | async-done | bytes 2359312 | tf_op jit(solution)/shard_map/reduce_scatter | solution.py:522
  627.5 2.5 copy.77
  630.6 2.1 copy.51
  632.7 2.1 copy.50
  634.8 2.1 copy.49
  (174 shorter events, 17.5 us)
Async XLA Ops:
  7.2 68.6 %copy-start = (bf16[192,768]{1,0:T(8,128)(2,1)S(1)}, bf16[192,768]{1,0:T(8,128)(2,1)}, u32[]{:S(2)}) copy-start(bf16[192,768]{1,0:T(8,128)(2,1)} %param.25) | copy-start | bytes 884740
  7.2 45.3 %copy-start.23 = (bf16[768,192]{0,1:T(8,128)(2,1)S(1)}, bf16[768,192]{0,1:T(8,128)(2,1)}, u32[]{:S(2)}) copy-start(bf16[768,192]{0,1:T(8,128)(2,1)} %param.22) | copy-start | bytes 884740
  7.2 43.2 %all-gather.5.cloned.1.call-start = ((), (), s32[]{:S(2)}) async-start(), calls=%async_computation.7 | async-start | bytes 1966080 | tf_op jit(solution)/shard_map/all_gather | solution.py:411
  8.5 2.6 copy-start.35
  8.5 2.6 copy-start.32
  10.4 101.5 %reduce-scatter.8.cloned.1.call-start = ((), (), s32[]{:S(2)}) async-start(), calls=%async_computation.8 | async-start | bytes 1966080 | tf_op jit(solution)/shard_map/reduce_scatter | solution.py:427
  11.1 43.9 %copy-start.19 = (f32[1024,32]{0,1:T(8,128)}, f32[1024,32]{0,1:T(8,128)S(1)}, u32[]{:S(2)}) copy-start(f32[1024,32]{0,1:T(8,128)S(1)} %get-tuple-element.480) | copy-start | bytes 393220
  11.1 43.9 %copy-start.21 = (f32[1024,32]{0,1:T(8,128)}, f32[1024,32]{0,1:T(8,128)S(1)}, u32[]{:S(2)}) copy-start(f32[1024,32]{0,1:T(8,128)S(1)} %get-tuple-element.481) | copy-start | bytes 393220
  52.5 2.6 copy-start.4
  52.5 2.6 copy-start.26
  55.0 1.5 copy-start.16
  55.0 1.5 copy-start.17
  75.3 3.2 copy-start.37
  75.3 36.7 %copy-start.6 = (bf16[256,768]{1,0:T(8,128)(2,1)S(1)}, bf16[256,768]{1,0:T(8,128)(2,1)}, u32[]{:S(2)}) copy-start(bf16[256,768]{1,0:T(8,128)(2,1)} %param.20) | copy-start | bytes 1179652
  75.3 37.9 %copy-start.8 = (bf16[256,768]{1,0:T(8,128)(2,1)S(1)}, bf16[256,768]{1,0:T(8,128)(2,1)}, u32[]{:S(2)}) copy-start(bf16[256,768]{1,0:T(8,128)(2,1)} %param.35) | copy-start | bytes 1179652
  75.3 37.9 %copy-start.31 = (f32[768]{0:T(1024)S(1)}, f32[768]{0:T(1024)}, u32[]{:S(2)}) copy-start(f32[768]{0:T(1024)} %param.26) | copy-start | bytes 9220
  75.8 39.5 %copy-start.12 = (bf16[24,8,2,512]{3,1,2,0:T(8,128)(2,1)}, bf16[24,8,2,512]{3,1,2,0:T(8,128)(2,1)S(1)}, u32[]{:S(2)}) copy-start(bf16[24,8,2,512]{3,1,2,0:T(8,128)(2,1)S(1)} %copy.75) | copy-start | bytes 1179652
  75.8 40.1 %copy-start.28 = (f32[768,12]{0,1:T(8,128)S(1)}, f32[768,12]{0,1:T(8,128)}, u32[]{:S(2)}) copy-start(f32[768,12]{0,1:T(8,128)} %param.27) | copy-start | bytes 110596
  75.8 40.1 %copy-start.29 = (f32[1024,12]{0,1:T(8,128)S(1)}, f32[1024,12]{0,1:T(8,128)}, u32[]{:S(2)}) copy-start(f32[1024,12]{0,1:T(8,128)} %param.28) | copy-start | bytes 147460
  75.8 111.8 %copy-start.3 = (s32[1024,2]{0,1:T(2,128)S(1)}, s32[1024,2]{0,1:T(2,128)}, u32[]{:S(2)}) copy-start(s32[1024,2]{0,1:T(2,128)} %param.34) | copy-start | bytes 24580
  77.6 72.0 %all-gather.9.cloned.1.call-start = ((), (), s32[]{:S(2)}) async-start(), calls=%async_computation.10 | async-start | bytes 1966080 | tf_op jit(solution)/shard_map/all_gather | solution.py:436
  78.4 109.2 %all-gather.7.cloned.1.call-start = ((), (), s32[]{:S(2)}) async-start(), calls=%async_computation.9 | async-start | bytes 1966080 | tf_op jit(solution)/shard_map/all_gather | solution.py:433
  115.3 133.9 %reduce-scatter.14.cloned.1.call-start = ((), (), s32[]{:S(2)}) async-start(), calls=%async_computation.13 | async-start | bytes 40960 | tf_op jit(solution)/shard_map/reduce_scatter | solution.py:456
  187.6 1.4 copy-start.2
  189.0 42.9 %copy-start.34 = (f32[2,768,2]{1,2,0:T(2,128)S(1)}, f32[2,768,2]{1,2,0:T(2,128)}, u32[]{:S(2)}) copy-start(f32[2,768,2]{1,2,0:T(2,128)} %param.29) | copy-start | bytes 36868
  189.0 43.1 %copy-start.7 = (bf16[256,768]{1,0:T(8,128)(2,1)S(1)}, bf16[256,768]{1,0:T(8,128)(2,1)}, u32[]{:S(2)}) copy-start(bf16[256,768]{1,0:T(8,128)(2,1)} %get-tuple-element.442) | copy-start | bytes 1179652
  189.0 96.5 %copy-start.9 = (bf16[256,768]{1,0:T(8,128)(2,1)S(1)}, bf16[256,768]{1,0:T(8,128)(2,1)}, u32[]{:S(2)}) copy-start(bf16[256,768]{1,0:T(8,128)(2,1)} %reduce-scatter.8.cloned.1.call-done) | copy-start | bytes 1179652
  231.3 54.3 %reduce-scatter.12.cloned.1.call-start = ((), (), s32[]{:S(2)}) async-start(), calls=%async_computation.12 | async-start | bytes 1966080 | tf_op jit(solution)/shard_map/reduce_scatter | solution.py:453
  231.9 94.1 %all-gather.11.cloned.1.call-start = ((), (), s32[]{:S(2)}) async-start(), calls=%async_computation.14 | async-start | bytes 1966080 | tf_op jit(solution)/shard_map/all_gather | solution.py:476
  287.7 0.9 copy-start.14
  289.7 132.7 %reduce-scatter.18.cloned.1.call-start = ((), (), s32[]{:S(2)}) async-start(), calls=%async_computation.16 | async-start | bytes 1327104 | tf_op jit(solution)/shard_map/reduce_scatter | solution.py:515
  328.7 52.7 %copy-start.20 = (f32[1024,32]{0,1:T(8,128)S(1)}, f32[1024,32]{0,1:T(8,128)}, u32[]{:S(2)}) copy-start(f32[1024,32]{0,1:T(8,128)} %copy-done.19) | copy-start | bytes 393220
  328.7 52.7 %copy-start.22 = (f32[1024,32]{0,1:T(8,128)S(1)}, f32[1024,32]{0,1:T(8,128)}, u32[]{:S(2)}) copy-start(f32[1024,32]{0,1:T(8,128)} %copy-done.21) | copy-start | bytes 393220
  377.3 5.6 copy-start.13
  380.1 2.9 copy-start.18
  381.4 2.1 copy-start.5
  383.0 1.5 copy-start.11
  385.1 1.8 copy-start.24
  386.6 1.9 copy-start.25
  386.6 2.5 copy-start.27
  386.6 74.0 %reduce-scatter.16.cloned.1.call-start = ((), (), s32[]{:S(2)}) async-start(), calls=%async_computation.15 | async-start | bytes 1966080 | tf_op jit(solution)/shard_map/reduce_scatter | solution.py:503
  391.0 114.5 %reduce-scatter.10.cloned.1.call-start = ((), (), s32[]{:S(2)}) async-start(), calls=%async_computation.11 | async-start | bytes 1966080 | tf_op jit(solution)/shard_map/reduce_scatter | solution.py:450
  391.6 235.9 %reduce-scatter.20.cloned.1.call-start = ((), (), s32[]{:S(2)}) async-start(), calls=%async_computation.17 | async-start | bytes 21233664 | tf_op jit(solution)/shard_map/reduce_scatter | solution.py:522
  421.5 39.1 %copy-start.30 = (f32[768]{0:T(1024)S(1)}, f32[768]{0:T(1024)}, u32[]{:S(2)}) copy-start(f32[768]{0:T(1024)} %param.21) | copy-start | bytes 9220
  421.5 39.1 %copy-start.33 = (f32[256]{0:T(256)S(1)}, f32[256]{0:T(256)}, u32[]{:S(2)}) copy-start(f32[256]{0:T(256)} %copy-done.32) | copy-start | bytes 3076
  421.5 83.9 %copy-start.36 = (f32[256]{0:T(256)S(1)}, f32[256]{0:T(256)}, u32[]{:S(2)}) copy-start(f32[256]{0:T(256)} %copy-done.35) | copy-start | bytes 3076
  421.5 83.9 %copy-start.10 = (bf16[256,768]{1,0:T(8,128)(2,1)S(1)}, bf16[256,768]{1,0:T(8,128)(2,1)}, u32[]{:S(2)}) copy-start(bf16[256,768]{1,0:T(8,128)(2,1)} %reduce-scatter.8.cloned.1.call-done) | copy-start | bytes 1179652
  421.5 83.9 %copy-start.15 = (f32[256,768]{1,0:T(8,128)S(1)}, f32[256,768]{1,0:T(8,128)}, u32[]{:S(2)}) copy-start(f32[256,768]{1,0:T(8,128)} %copy-done.14) | copy-start | bytes 2359300
  632.7 4.1 copy-start.1
Sparse Core Ops, SparseCore 0:
  10.6 39.7 all-gather.4
  77.8 34.1 reduce-scatter.7
  113.5 36.0 all-gather.8
  151.6 35.9 all-gather.6
  231.4 17.7 reduce-scatter.13
  252.0 33.4 reduce-scatter.11
  289.8 36.0 all-gather.10
  386.7 35.6 reduce-scatter.17
  425.3 35.2 reduce-scatter.15
  463.3 35.3 reduce-scatter.9
  502.3 125.0 reduce-scatter.19

commit v2 on v1

v2 whole, which is shorter than its diff:
```python
import functools
import math

import jax
import jax.numpy as jnp
import numpy as np
from jax import lax
from jax.experimental import pallas as pl
from jax.experimental.pallas import tpu as pltpu
from jax.sharding import PartitionSpec as P

HD = 64
LENGTH = 1024
BLOCK = 256
CAP = 256


EPSILON = 1e-06
MASKED = -1e30


def rope_tables(length, head_width):
    position = jnp.arange(length, dtype=jnp.float32)[:, None]
    inverse = jnp.exp(
        jnp.arange(head_width // 2, dtype=jnp.float32) * (-2.0 * math.log(10000.0) / head_width)
    )
    angle = position * inverse[None, :]
    return (jnp.cos(angle), jnp.sin(angle))


def rotate(values, cosine, sine):
    half_width = values.shape[-1] // 2
    first_half = values[..., :half_width]
    second_half = values[..., half_width:]
    cos_table = cosine[:, None, :]
    sin_table = sine[:, None, :]
    return jnp.concatenate(
        [
            first_half * cos_table - second_half * sin_table,
            second_half * cos_table + first_half * sin_table,
        ],
        axis=-1,
    )


def unrotate(values, cosine, sine):
    half_width = values.shape[-1] // 2
    first_half = values[..., :half_width]
    second_half = values[..., half_width:]
    cos_table = cosine[:, None, :]
    sin_table = sine[:, None, :]
    return jnp.concatenate(
        [
            first_half * cos_table + second_half * sin_table,
            second_half * cos_table - first_half * sin_table,
        ],
        axis=-1,
    )


def rms_norm(values, gain):
    scale = lax.rsqrt(jnp.mean(values * values, axis=-1, keepdims=True) + EPSILON)
    return values * scale * gain


def block_mask(query_start, query_rows, length):
    query_pos = query_start + jnp.arange(query_rows, dtype=jnp.int32)
    key_pos = jnp.arange(length, dtype=jnp.int32)
    return (key_pos // BLOCK)[None, :] <= (query_pos // BLOCK)[:, None]


def attention_forward(query, key, value):
    seq_count, length, head_count, head_width = query.shape
    query_rows = min(512, length)
    block_count = length // query_rows
    scale = head_width ** (-0.5)

    def one_block(block_index):
        seq_index = block_index // block_count
        query_start = block_index % block_count * query_rows
        query_seq = lax.dynamic_index_in_dim(query, seq_index, 0, keepdims=False)
        query_blk = lax.dynamic_slice_in_dim(query_seq, query_start, query_rows, 0)
        key_seq = lax.dynamic_index_in_dim(key, seq_index, 0, keepdims=False)
        value_seq = lax.dynamic_index_in_dim(value, seq_index, 0, keepdims=False)
        scores = (
            jnp.einsum("qhd,khd->hqk", query_blk, key_seq, preferred_element_type=jnp.float32)
            * scale
        )
        scores = jnp.where(block_mask(query_start, query_rows, length)[None], scores, MASKED)
        row_max = jnp.max(scores, axis=-1, keepdims=True)
        exp_scores = jnp.exp(scores - row_max)
        row_total = jnp.sum(exp_scores, axis=-1, keepdims=True)
        soft_probs = (exp_scores / row_total).astype(jnp.bfloat16)
        result = jnp.einsum(
            "hqk,khd->qhd", soft_probs, value_seq, preferred_element_type=jnp.float32
        )
        return (result, (row_max + jnp.log(row_total))[..., 0])

    return lax.map(one_block, jnp.arange(seq_count * block_count, dtype=jnp.int32))


EXP_PAD = 16


def dot(a, b):
    return jnp.dot(a, b, preferred_element_type=jnp.float32)


def dot_nt(a, b):
    return lax.dot_general(a, b, (((1,), (1,)), ((), ())), preferred_element_type=jnp.float32)


def dot_tn(a, b):
    return lax.dot_general(a, b, (((0,), (0,)), ((), ())), preferred_element_type=jnp.float32)


def three_parts(values):
    first = values.astype(jnp.bfloat16)
    rest = values - first.astype(jnp.float32)
    second = rest.astype(jnp.bfloat16)
    third = (rest - second.astype(jnp.float32)).astype(jnp.bfloat16)
    return (first, second, third)


def expert_kernel(
    n_dp,
    ffn_count,
    route_count,
    moe_ref,
    grad_ref,
    routes_ref,
    residual_ref,
    router_ref,
    gate_ref,
    up_ref,
    down_ref,
    part_ref,
    back_ref,
    chosen_ref,
    weight_ref,
    probs_s,
    rank_s,
    part_s,
    back_s,
):
    expert = pl.program_id(0)
    rows = moe_ref.shape[0]
    hidden = gate_ref.shape[2]
    step = moe_ref.shape[1] // n_dp

    @pl.when(expert == 0)
    def _():
        parts = three_parts(router_ref[...])
        logits = residual_ref[...]
        for part in parts:
            logits = logits + dot_nt(part, moe_ref[...])
        index = lax.broadcasted_iota(jnp.int32, (EXP_PAD, rows), 0)
        logits = jnp.where(index < route_count, logits, MASKED)
        top = jnp.max(logits, axis=0, keepdims=True)
        exps = jnp.exp(logits - top)
        probs_s[...] = exps / jnp.sum(exps, axis=0, keepdims=True)
        named = (routes_ref[0:1, :] == index) | (routes_ref[1:2, :] == index)
        named = jnp.where(named, 1.0, 0.0)
        width = 256
        before = lax.broadcasted_iota(jnp.int32, (width, width), 0)
        after = lax.broadcasted_iota(jnp.int32, (width, width), 1)
        earlier = jnp.where(before < after, 1.0, 0.0).astype(jnp.bfloat16)
        total = jnp.zeros((EXP_PAD, 1), jnp.float32)
        for start in range(0, rows, width):
            block = named[:, start : start + width]
            rank = dot(block.astype(jnp.bfloat16), earlier) + total
            rank_s[:, start : start + width] = jnp.where(block > 0.5, rank, -1.0)
            total = total + jnp.sum(block, axis=1, keepdims=True)
        part_s[...] = jnp.zeros_like(part_s)
        back_s[...] = jnp.zeros_like(back_s)

    slot = lax.broadcasted_iota(jnp.int32, (CAP, rows), 0).astype(jnp.float32)
    hit = rank_s[pl.ds(expert, 1), :] == slot
    dispatch = jnp.where(hit, 1.0, 0.0).astype(jnp.bfloat16)
    slot_weight = jnp.sum(
        jnp.where(hit, probs_s[pl.ds(expert, 1), :], 0.0), axis=1, keepdims=True
    )
    rows_in = dot(dispatch, moe_ref[...]).astype(jnp.bfloat16)
    rows_grad = dot(dispatch, grad_ref[...])
    gate_w = gate_ref[0]
    up_w = up_ref[0]
    down_w = down_ref[0]
    gate_pre = dot(rows_in, gate_w)
    up_pre = dot(rows_in, up_w)
    sigmoid = 1.0 / (1.0 + jnp.exp(-gate_pre))
    silu = gate_pre * sigmoid
    active = (silu * up_pre).astype(jnp.bfloat16)
    out = dot(active, down_w)
    inner = jnp.sum(rows_grad * out, axis=1, keepdims=True)
    chosen_row = jnp.sum(jnp.where(hit, inner, 0.0), axis=0, keepdims=True)
    for n in range(chosen_ref.shape[0]):
        chosen_ref[n, pl.ds(expert, 1), :] = chosen_row[
            :, n * chosen_ref.shape[2] : (n + 1) * chosen_ref.shape[2]
        ]
    part_s[...] += dot_tn(dispatch, (out * slot_weight).astype(jnp.bfloat16))
    grad_low = (rows_grad * slot_weight).astype(jnp.bfloat16)
    grad_active = dot_nt(grad_low, down_w)
    grad_gate = (grad_active * up_pre * sigmoid * (1.0 + gate_pre * (1.0 - sigmoid))).astype(
        jnp.bfloat16
    )
    grad_up = (grad_active * silu).astype(jnp.bfloat16)
    grad_in = dot_nt(grad_gate, gate_w) + dot_nt(grad_up, up_w)
    back_s[...] += dot_tn(dispatch, grad_in.astype(jnp.bfloat16))
    for n, (left, right) in enumerate(
        ((rows_in, grad_gate), (rows_in, grad_up), (grad_low, active))
    ):
        product = dot_tn(left, right).astype(jnp.bfloat16)
        for d in range(n_dp):
            weight_ref[0, d % 2, d // 2, :, n * hidden : (n + 1) * hidden] = product[
                d * step : (d + 1) * step
            ]

    @pl.when(expert == ffn_count - 1)
    def _():
        part_ref[...] = part_s[...].astype(jnp.bfloat16)
        back_ref[...] = back_s[...].astype(jnp.bfloat16)


def experts(n_dp, n_t, route_count, moe_rows, grad_rows, routes_t, residual_t, router_t, gate_w, up_w, down_w):
    rows, width = moe_rows.shape
    ffn_count, _, hidden = gate_w.shape
    step = width // n_dp

    def whole(shape):
        return pl.BlockSpec(shape, lambda e: (0,) * len(shape), pipeline_mode=pl.Buffered(1))

    return pl.pallas_call(
        functools.partial(expert_kernel, n_dp, ffn_count, route_count),
        grid=(ffn_count,),
        out_shape=(
            jax.ShapeDtypeStruct((rows, width), jnp.bfloat16),
            jax.ShapeDtypeStruct((rows, width), jnp.bfloat16),
            jax.ShapeDtypeStruct((n_t, ffn_count, rows // n_t), jnp.float32),
            jax.ShapeDtypeStruct((ffn_count, 2, n_dp // 2, step, 3 * hidden), jnp.bfloat16),
        ),
        in_specs=[
            whole((rows, width)),
            whole((rows, width)),
            whole((2, rows)),
            whole((EXP_PAD, rows)),
            whole((EXP_PAD, width)),
            pl.BlockSpec((1, width, hidden), lambda e: (e, 0, 0)),
            pl.BlockSpec((1, width, hidden), lambda e: (e, 0, 0)),
            pl.BlockSpec((1, hidden, width), lambda e: (e, 0, 0)),
        ],
        out_specs=(
            whole((rows, width)),
            whole((rows, width)),
            whole((n_t, ffn_count, rows // n_t)),
            pl.BlockSpec((1, 2, n_dp // 2, step, 3 * hidden), lambda e: (e, 0, 0, 0, 0)),
        ),
        scratch_shapes=[
            pltpu.VMEM((EXP_PAD, rows), jnp.float32),
            pltpu.VMEM((EXP_PAD, rows), jnp.float32),
            pltpu.VMEM((rows, width), jnp.float32),
            pltpu.VMEM((rows, width), jnp.float32),
        ],
        compiler_params=pltpu.CompilerParams(
            dimension_semantics=("arbitrary",), vmem_limit_bytes=48 << 20
        ),
        name="experts",
    )(moe_rows, grad_rows, routes_t, residual_t, router_t, gate_w, up_w, down_w)


MESH = pl.DeviceIdType.MESH


def bit_of(index, position):
    return index // (1 << position) % 2


def flipped(index, position):
    return index + (1 << position) * (1 - 2 * bit_of(index, position))


def log2_of(count):
    return count.bit_length() - 1


def greet(dp, place, dp_bits, tensor_count):
    barrier = pltpu.get_barrier_semaphore()
    for position in range(dp_bits):
        pl.semaphore_signal(
            barrier, inc=1, device_id={"dp": flipped(dp, position)}, device_id_type=MESH
        )
    for step in range(1, tensor_count):
        pl.semaphore_signal(
            barrier,
            inc=1,
            device_id={"tensor": (place + step) % tensor_count},
            device_id_type=MESH,
        )
    pl.semaphore_wait(barrier, dp_bits + tensor_count - 1)


class LineGather:
    def __init__(self, blocks, send, recv, place):
        self.blocks, self.send, self.recv, self.place = blocks, send, recv, place
        self.count = blocks.shape[0]

    def copy(self, block, way):
        return pltpu.make_async_remote_copy(
            src_ref=self.blocks.at[block],
            dst_ref=self.blocks.at[block],
            send_sem=self.send.at[way, block],
            recv_sem=self.recv.at[block],
            device_id={"tensor": self.place + 1 - 2 * way},
            device_id_type=MESH,
        )

    def start(self):
        self.pass_on(self.place)

    def pass_on(self, block, ways=(0, 1)):
        if 0 in ways:

            @pl.when(self.place < self.count - 1)
            def _():
                self.copy(block, 0).start()

        if 1 in ways:

            @pl.when(self.place > 0)
            def _():
                self.copy(block, 1).start()

    def step(self, distance):
        below, above = self.place - distance, self.place + distance

        @pl.when(below >= 0)
        def _():
            self.copy(below, 0).wait_recv()
            self.pass_on(below, (0,))

        @pl.when(above < self.count)
        def _():
            self.copy(above, 1).wait_recv()
            self.pass_on(above, (1,))

    def finish(self):
        for distance in range(self.count):
            below, above = self.place - distance, self.place + distance

            @pl.when((below >= 0) & (self.place < self.count - 1))
            def _(below=below):
                self.copy(below, 0).wait_send()

            @pl.when((above < self.count) & (self.place > 0))
            def _(above=above):
                self.copy(above, 1).wait_send()


class LineScatter:
    def __init__(self, parts, arrived, send, recv, place, pieces):
        self.parts, self.arrived, self.send, self.recv = parts, arrived, send, recv
        self.place, self.count, self.pieces = place, parts.shape[0], pieces
        self.rows = parts.shape[1] // pieces

    def piece(self, ref, block, n):
        return ref.at[block, pl.ds(n * self.rows, self.rows)]

    def copy(self, block, n, way, own=False):
        there = self.piece(self.arrived, block + 1 - way, n)
        return pltpu.make_async_remote_copy(
            src_ref=self.piece(self.parts, block, n) if own else there,
            dst_ref=there,
            send_sem=self.send.at[way, block, n],
            recv_sem=self.recv.at[way, block, n],
            device_id={"tensor": self.place + 1 - 2 * way},
            device_id_type=MESH,
        )

    def originate(self, block):
        for way, first in ((0, 0), (1, self.count - 1)):
            if block != first:

                @pl.when(self.place == first)
                def _(way=way):
                    for n in range(self.pieces):
                        self.copy(block, n, way, own=True).start()

    def forward(self, block):
        for way in (0, 1):
            inside = (
                (self.place > 0) & (self.place < block)
                if way == 0
                else (self.place > block) & (self.place < self.count - 1)
            )

            @pl.when(inside)
            def _(way=way):
                for n in range(self.pieces):
                    self.copy(block, n, way).wait_recv()
                    there = self.piece(self.arrived, block + 1 - way, n)
                    mine = self.piece(self.parts, block, n)
                    there[...] = (
                        there[...].astype(jnp.float32) + mine[...].astype(jnp.float32)
                    ).astype(there.dtype)
                    self.copy(block, n, way).start()

    def collect(self, total):
        place = self.place
        total[...] = self.parts[place].astype(jnp.float32)
        for way in (0, 1):

            @pl.when(place > 0 if way == 0 else place < self.count - 1)
            def _(way=way):
                for n in range(self.pieces):
                    self.copy(place, n, way).wait_recv()
                    rows = pl.ds(n * self.rows, self.rows)
                    total[rows, :] += self.arrived[place + 1 - way, rows, :].astype(jnp.float32)

    def finish(self):
        for block in range(self.count):
            for way in (0, 1):

                @pl.when(self.place < block if way == 0 else self.place > block)
                def _(block=block, way=way):
                    for n in range(self.pieces):
                        self.copy(block, n, way).wait_send()


class Halving:
    def __init__(self, source, kept, first, stages, sems, dp, dp_bits, splits):
        self.source, self.kept, self.first, self.stages = source, kept, first, stages
        self.first_send, self.first_recv, self.local, self.send, self.recv = sems
        self.dp, self.bits, self.splits = dp, dp_bits, splits
        self.core = bit_of(dp, 0)
        upper = list(range(dp_bits - 1))
        self.orders = (upper, upper[1:] + upper[:1])

    def first_copy(self, e):
        return pltpu.make_async_remote_copy(
            src_ref=self.source.at[e, 1 - self.core],
            dst_ref=self.first.at[e],
            send_sem=self.first_send.at[e],
            recv_sem=self.first_recv.at[e],
            device_id={"dp": flipped(self.dp, 0)},
            device_id_type=MESH,
        )

    def local_copy(self, e):
        return pltpu.make_async_copy(
            self.source.at[e, self.core], self.kept.at[e], self.local.at[e]
        )

    def blocks(self, part, stage, k, mine):
        order = self.orders[part]
        index = 0
        for done in order[:stage]:
            index = index + (1 << done) * bit_of(self.dp, done + 1)
        here = bit_of(self.dp, order[stage] + 1)
        index = index + (1 << order[stage]) * (here if mine else 1 - here)
        for n, free in enumerate(order[stage + 1 :]):
            index = index + (1 << free) * (k // (1 << n) % 2)
        return index

    def width(self, part):
        return pl.ds(*self.splits[part])

    def stage_copy(self, e, part, stage, k):
        start, size = self.splits[part]
        return pltpu.make_async_remote_copy(
            src_ref=self.kept.at[e, self.blocks(part, stage, k, False), :, pl.ds(start, size)],
            dst_ref=self.stages[stage].at[e, k, :, pl.ds(start, size)],
            send_sem=self.send[stage].at[e, part, k],
            recv_sem=self.recv[stage].at[e, part, k],
            device_id={"dp": flipped(self.dp, self.orders[part][stage] + 1)},
            device_id_type=MESH,
        )

    def number(self, stage):
        return 1 << (self.bits - 2 - stage)

    def start(self, e):
        self.first_copy(e).start()
        self.local_copy(e).start()

    def send_stage(self, e, stage):
        for k in range(self.number(stage)):
            for part in (0, 1):
                self.stage_copy(e, part, stage, k).start()

    def add_rows(self, target, addend):
        rows = target.shape[0]
        step = 32 if rows % 32 == 0 else rows

        def body(n, _):
            at = pl.ds(pl.multiple_of(n * step, step), step)
            target[at, :] = (
                target[at, :].astype(jnp.float32) + addend[at, :].astype(jnp.float32)
            ).astype(target.dtype)
            return 0

        lax.fori_loop(0, rows // step, body, 0)

    def open(self, e, remote_only=False):
        self.first_copy(e).wait_recv()
        if not remote_only:
            self.local_copy(e).wait()
        for block in range(self.kept.shape[1]):
            self.add_rows(self.kept.at[e, block], self.first.at[e, block])
        self.send_stage(e, 0)

    def advance(self, e, stage):
        for k in range(self.number(stage)):
            for part in (0, 1):
                self.stage_copy(e, part, stage, k).wait_recv()
                block = self.blocks(part, stage, k, True)
                self.add_rows(
                    self.kept.at[e, block, :, self.width(part)],
                    self.stages[stage].at[e, k, :, self.width(part)],
                )
        self.send_stage(e, stage + 1)

    def close(self, e, out):
        stage = self.bits - 2
        for part in (0, 1):
            self.stage_copy(e, part, stage, 0).wait_recv()
            block = self.blocks(part, stage, 0, True)
            columns = self.width(part)
            out[:, columns] = self.kept[e, block, :, columns].astype(jnp.float32) + self.stages[
                stage
            ][e, 0, :, columns].astype(jnp.float32)

    def finish(self, e):
        self.first_copy(e).wait_send()
        for stage in range(self.bits - 1):
            for k in range(self.number(stage)):
                for part in (0, 1):
                    self.stage_copy(e, part, stage, k).wait_send()


class Butterfly:
    def __init__(self, total, arrived, send, recv, dp, place, dp_bits, tensor_bits):
        self.total, self.arrived, self.send, self.recv = total, arrived, send, recv
        self.partners = [{"dp": flipped(dp, b)} for b in range(dp_bits)]
        self.partners += [{"tensor": flipped(place, b)} for b in range(tensor_bits)]

    def copy(self, n):
        return pltpu.make_async_remote_copy(
            src_ref=self.total,
            dst_ref=self.arrived.at[n],
            send_sem=self.send.at[n],
            recv_sem=self.recv.at[n],
            device_id=self.partners[n],
            device_id_type=MESH,
        )

    def start(self, n):
        self.copy(n).start()

    def take(self, n):
        self.copy(n).wait()
        self.total[...] += self.arrived[n]


def side_forward(norm, named, residual, weight_parts, const_value, route_count, ffn_count):
    lane = lax.broadcasted_iota(jnp.int32, named.shape, 1)
    low = norm.astype(jnp.bfloat16)
    both = dot(low, weight_parts[0]) + dot(low, weight_parts[1]) + dot(low, weight_parts[2])
    logits = jnp.where(lane < route_count, both + residual, MASKED)
    exps = jnp.exp(logits - jnp.max(logits, axis=1, keepdims=True))
    probs = exps / jnp.sum(exps, axis=1, keepdims=True)
    chosen = probs * named
    shares, keeps, rests = [], chosen[:, ffn_count + 1 : ffn_count + 2], []
    for c in range(2):
        at = route_count + 2 * c
        share = 1.0 / (1.0 + jnp.exp(both[:, at + 1 : at + 2] - both[:, at : at + 1]))
        weight = chosen[:, ffn_count + 2 + c : ffn_count + 3 + c]
        shares.append(share)
        keeps = keeps + weight * share
        rests.append(weight * (1.0 - share))
    special = keeps * norm + rests[0] * const_value[0:1] + rests[1] * const_value[1:2]
    return probs, chosen, shares, keeps, rests, special


def side_backward(
    norm, grad, named, forward, chosen_back, weight_parts, const_value, route_count, ffn_count
):
    probs, chosen, shares, keeps, rests, _ = forward
    lane = lax.broadcasted_iota(jnp.int32, named.shape, 1)
    self_dot = jnp.sum(grad * norm, axis=1, keepdims=True)
    value_dots = [
        jnp.sum(grad * const_value[c : c + 1], axis=1, keepdims=True) for c in range(2)
    ]
    d_probs = jnp.where(lane < ffn_count, chosen_back, 0.0)
    d_probs = jnp.where(lane == ffn_count + 1, self_dot, d_probs)
    for c in range(2):
        mixed = shares[c] * self_dot + (1.0 - shares[c]) * value_dots[c]
        d_probs = jnp.where(lane == ffn_count + 2 + c, mixed, d_probs)
    d_probs = d_probs * named
    d_both = probs * (d_probs - jnp.sum(probs * d_probs, axis=1, keepdims=True))
    d_both = jnp.where(lane < route_count, d_both, 0.0)
    for c in range(2):
        weight = chosen[:, ffn_count + 2 + c : ffn_count + 3 + c]
        d_share = shares[c] * (1.0 - shares[c]) * weight * (self_dot - value_dots[c])
        d_both = jnp.where(lane == route_count + 2 * c, d_share, d_both)
        d_both = jnp.where(lane == route_count + 2 * c + 1, -d_share, d_both)
    d_parts = three_parts(d_both)
    back = keeps * grad
    for m, n in ((0, 0), (0, 1), (1, 0), (1, 1)):
        back = back + dot_nt(d_parts[m], weight_parts[n])
    low = norm.astype(jnp.bfloat16)
    weight_part = dot_tn(d_parts[0], low) + dot_tn(d_parts[1], low) + dot_tn(d_parts[2], low)
    value_part = [jnp.sum(rests[c] * grad, axis=0, keepdims=True) for c in range(2)]
    return back, weight_part, value_part


class Nothing:
    def __getattr__(self, name):
        return lambda *arguments: None


def reduced_inside(step):
    return step % 32 == 0


def backward_kernel(
    sizes,
    part_ref,
    back_ref,
    chosen_ref,
    expert_ref,
    hidden_ref,
    moe_ref,
    grad_ref,
    input_ref,
    routes_ref,
    residual_ref,
    both_ref,
    value_ref,
    moe_gain_ref,
    attn_gain_ref,
    q_ref,
    k_ref,
    v_ref,
    o_ref,
    lse_ref,
    rows_ref,
    qkv_ref,
    out_w_ref,
    table_ref,
    output_ref,
    input_grad_ref,
    expert_out,
    attn_out,
    small_out,
    gain_out,
    chosen_in,
    pair_buf,
    line_back,
    line_part,
    staged,
    grad_rows,
    attn_part,
    acc,
    hidden_grad,
    double_grad,
    delta,
    dq,
    dk,
    dv,
    packed,
    *rest,
):
    dp_bits, n_t, ffn_count, route_count, attn_split, inside = sizes
    stage_count = dp_bits - 1 if inside else 0
    if inside:
        attn_pairs, kept, first = rest[:3]
        stages = rest[3 : 3 + stage_count]
        rest = rest[3 + stage_count :]
        a_kept, a_first = rest[:2]
        a_stages = rest[2 : 2 + stage_count]
        rest = rest[2 + stage_count :]
    else:
        attn_pairs = attn_out
    small_in, gain_acc, gain_in = rest[:3]
    rest = list(rest[3:])

    def sems(count):
        taken = rest[:count]
        del rest[:count]
        return taken

    (chosen_send, chosen_recv, gather_send, gather_recv) = sems(4)
    line_sems = [sems(2) for _ in range(3)]
    if inside:
        e_sems = sems(3) + [sems(stage_count), sems(stage_count)]
        a_sems = sems(3) + [sems(stage_count), sems(stage_count)]
    small_sems = sems(2)
    gain_sems = sems(2)
    (staged_sem,) = sems(1)

    dp = lax.axis_index("dp")
    place = lax.axis_index("tensor")
    local = hidden_ref.shape[0]
    width = hidden_ref.shape[1]
    hidden_units = expert_ref.shape[-1]
    heads = q_ref.shape[0]
    tensor_bits = log2_of(n_t)
    greet(dp, place, dp_bits, n_t)

    back_line = LineScatter(back_ref, line_back, *line_sems[0], place, 2)
    part_line = LineScatter(part_ref, line_part, *line_sems[1], place, 2)
    attn_line = LineScatter(attn_part, line_back, *line_sems[2], place, 4)
    gather = LineGather(grad_rows, gather_send, gather_recv, place)
    half = hidden_units // 2
    attn_width = attn_pairs.shape[-1]
    expert = attn = Nothing()
    if inside:
        splits = ((0, half), (half, half))
        expert = Halving(expert_ref, kept, first, stages, e_sems, dp, dp_bits, splits)
        splits = ((0, attn_split), (attn_split, attn_width - attn_split))
        attn = Halving(attn_pairs, a_kept, a_first, a_stages, a_sems, dp, dp_bits, splits)
    small = Butterfly(small_out, small_in, *small_sems, dp, place, dp_bits, tensor_bits)
    gain = Butterfly(gain_acc, gain_in, *gain_sems, dp, place, dp_bits, tensor_bits)

    def chosen_copy(step):
        there = (place + step) % n_t
        return pltpu.make_async_remote_copy(
            src_ref=chosen_ref.at[there],
            dst_ref=chosen_in.at[step - 1],
            send_sem=chosen_send.at[step - 1],
            recv_sem=chosen_recv.at[step - 1],
            device_id={"tensor": there},
            device_id_type=MESH,
        )

    for block in (n_t - 1, 0, *range(n_t - 2, 0, -1)):
        back_line.originate(block)
    for step in range(1, n_t):
        chosen_copy(step).start()

    def begin(e, _):
        expert.start(e)
        return 0

    lax.fori_loop(0, ffn_count, begin, 0)

    norm = moe_ref[place].astype(jnp.float32)
    lane = lax.broadcasted_iota(jnp.int32, (local, 128), 1)
    routes = routes_ref[...]
    named = (routes[:, 0:1] == lane) | (routes[:, 1:2] == lane)
    named = jnp.where(named, 1.0, 0.0)
    residual = jnp.concatenate(
        [residual_ref[...], jnp.zeros((local, 128 - route_count), jnp.float32)], axis=1
    )
    weight_parts = three_parts(both_ref[...])
    const_value = value_ref[...]
    grad = grad_ref[...].astype(jnp.float32)
    forward = side_forward(
        norm, named, residual, weight_parts, const_value, route_count, ffn_count
    )
    hidden = hidden_ref[...]
    pair_buf[...] = hidden + forward[-1]

    for block in (n_t - 1, 0, *range(n_t - 2, 0, -1)):
        back_line.forward(block)
    for block in (n_t - 1, 0, *range(n_t - 2, 0, -1)):
        part_line.originate(block)

    def opened(e, _):
        expert.open(e)
        return 0

    lax.fori_loop(0, ffn_count, opened, 0)

    back_line.collect(acc)
    chosen_total = chosen_ref[place]
    for step in range(1, n_t):
        chosen_copy(step).wait_recv()
        chosen_total = chosen_total + chosen_in[step - 1]
    chosen_back = jnp.concatenate(
        [chosen_total, jnp.zeros((128 - ffn_count, local), jnp.float32)], axis=0
    ).T
    back, weight_part, value_part = side_backward(
        norm, grad, named, forward, chosen_back, weight_parts, const_value, route_count, ffn_count
    )
    norm_grad = acc[...] + back
    scale = lax.rsqrt(jnp.mean(hidden * hidden, axis=1, keepdims=True) + EPSILON)
    u = norm_grad * moe_gain_ref[...]
    small_out[0:1, :] = jnp.sum(norm_grad * hidden * scale, axis=0, keepdims=True)
    small_out[1:2, :] = value_part[0]
    small_out[2:3, :] = value_part[1]
    small_out[3:8, :] = jnp.zeros((5, width), jnp.float32)
    small_out[8:24, :] = weight_part[0:16]
    hidden_grad[...] = (
        grad + scale * u - hidden * (scale * scale * scale) * jnp.mean(u * hidden, axis=1, keepdims=True)
    )
    grad_rows[place] = hidden_grad[...].astype(jnp.bfloat16)
    back_line.finish()
    gather.start()
    small.start(0)
    for block in (n_t - 1, 0, *range(n_t - 2, 0, -1)):
        part_line.forward(block)
    for step in range(1, n_t):
        gather.step(step)
        if step < small_in.shape[0]:
            small.take(step - 1)
            small.start(step)

    rows = local

    def row_block(n):
        return pl.ds(pl.multiple_of(n * rows, rows), rows)

    count = n_t
    head_lane = lax.broadcasted_iota(jnp.int32, (rows, 128), 1)
    low_half = head_lane < 64
    for block in range(count):
        at = pl.ds(block * rows, rows)
        product = dot_nt(grad_rows[block], out_w_ref[...])
        for h in range(heads):
            piece = product[:, h * 128 : (h + 1) * 128].astype(jnp.bfloat16)
            double_grad[h, at, :] = piece
            both = piece.astype(jnp.float32) * o_ref[h, at, :].astype(jnp.float32)
            delta[h : h + 1, at] = 0.5 * jnp.sum(both.T, axis=0, keepdims=True)
    out_pack = []
    for h in range(0, heads, 2):
        o_a = o_ref[h]
        o_b = o_ref[h + 1] if h + 1 < heads else jnp.zeros_like(o_a)
        lanes = lax.broadcasted_iota(jnp.int32, o_a.shape, 1)
        out_pack.append(jnp.where(lanes < 64, o_a, o_b))
    n_half = attn_pairs.shape[2]
    step_rows = attn_pairs.shape[3]
    qkv_width = packed.shape[1]

    def spread(product, start, stop):
        low = product.astype(jnp.bfloat16)
        for d in range(2 * n_half):
            attn_pairs[0, d % 2, d // 2, :, start:stop] = low[d * step_rows : (d + 1) * step_rows]

    for n, pack in enumerate(out_pack):
        total = jnp.zeros((width, 128), jnp.float32)
        for block in range(count):
            total = total + dot_tn(grad_rows[block], pack[block * rows : (block + 1) * rows])
        spread(total, qkv_width + n * 128, qkv_width + (n + 1) * 128)

    def advance_all(stage):
        def body(e, _):
            expert.advance(e, stage)
            return 0

        lax.fori_loop(0, ffn_count, body, 0)

    dq[...] = jnp.zeros_like(dq)
    factor = 64 ** (-0.5)
    gain_total = jnp.zeros((1, width), jnp.float32)
    for key_block in range(count):
        keys = pl.ds(key_block * rows, rows)
        dk[...] = jnp.zeros_like(dk)
        dv[...] = jnp.zeros_like(dv)

        def query_step(query_block, _, keys=keys):
            at = row_block(query_block)
            for h in range(heads):
                q, g = q_ref[h, at, :], double_grad[h, at, :]
                k, v = k_ref[h, keys, :], v_ref[h, keys, :]
                scores = dot_nt(k, q) * (0.5 * factor)
                probs = jnp.exp(scores - lse_ref[h : h + 1, at])
                d_probs = dot_nt(v, g) * 0.5
                d_scores = (probs * (d_probs - delta[h : h + 1, at])).astype(jnp.bfloat16)
                dk[h] += dot(d_scores, q)
                dv[h] += dot(probs.astype(jnp.bfloat16), g)
                dq[h, at, :] += dot_tn(d_scores, k)
            return 0

        lax.fori_loop(key_block, count, query_step, 0)
        table = table_ref[keys, :]
        pieces = []
        for source in (dq.at[:, keys, :], dk):
            for h in range(heads):
                turned = source[h] * (table * factor)
                pieces.append(turned + pltpu.roll(turned, 64, 1))
        for h in range(heads):
            pieces.append(dv[h])
        if len(pieces) % 2:
            pieces.append(jnp.zeros((rows, 128), jnp.float32))
        for n in range(0, len(pieces), 2):
            packed[keys, n * 64 : n * 64 + 128] = jnp.where(
                low_half, pieces[n], pieces[n + 1]
            ).astype(jnp.bfloat16)
        back_rows = dot_nt(packed[keys, :], qkv_ref[...])
        gain_total = gain_total + jnp.sum(
            back_rows * rows_ref[key_block].astype(jnp.float32), axis=0, keepdims=True
        )
        attn_part[key_block] = back_rows.astype(jnp.bfloat16)
        attn_line.originate(key_block)
        if key_block > 0:
            attn_line.forward(key_block - 1)
        if key_block == 0:
            part_line.collect(acc)
            output_ref[...] = (pair_buf[...] + acc[...]).astype(output_ref.dtype)

    gain_acc[...] = jnp.broadcast_to(gain_total / attn_gain_ref[...], gain_acc.shape)
    gain.start(0)
    for n in range(qkv_width // 128):
        total = jnp.zeros((width, 128), jnp.float32)
        for block in range(count):
            total = total + dot_tn(
                rows_ref[block], packed[pl.ds(block * rows, rows), n * 128 : (n + 1) * 128]
            )
        spread(total, n * 128, (n + 1) * 128)
    attn.start(0)
    attn_line.forward(count - 1)
    gain.take(0)
    gain.start(1)
    attn.open(0)
    for stage in range(stage_count - 1):
        advance_all(stage)
        attn.advance(0, stage)
    for n in range(1, gain_in.shape[0]):
        gain.take(n)
        if n + 1 < gain_in.shape[0]:
            gain.start(n + 1)
    for n in range(n_t - 1, small_in.shape[0]):
        small.take(n)
        if n + 1 < small_in.shape[0]:
            small.start(n + 1)
    gain_out[...] = gain_acc[...]
    attn_line.collect(acc)
    wide = input_ref[...].astype(jnp.float32)
    scale = lax.rsqrt(jnp.mean(wide * wide, axis=1, keepdims=True) + EPSILON)
    w = acc[...] * attn_gain_ref[...]
    input_grad_ref[...] = (
        hidden_grad[...]
        + scale * w
        - wide * (scale * scale * scale) * jnp.mean(w * wide, axis=1, keepdims=True)
    ).astype(input_grad_ref.dtype)
    def stored(e):
        return pltpu.make_async_copy(staged.at[e % 2], expert_out.at[e], staged_sem.at[e])

    for e in range(ffn_count if inside else 0):
        if e > 1:
            stored(e - 2).wait()
        expert.close(e, staged.at[e % 2])
        stored(e).start()
    attn.close(0, attn_out)

    for line in (part_line, attn_line):
        line.finish()
    for step in range(1, n_t):
        chosen_copy(step).wait_send()
    gather.finish()

    def ended(e, _):
        expert.finish(e)
        return 0

    lax.fori_loop(0, ffn_count, ended, 0)
    attn.finish(0)
    for e in range(ffn_count - 2, ffn_count if inside else 0):
        stored(e).wait()


def backward(dp_count, n_t, ffn_part, ffn_back, chosen, expert_part, hidden, moe_rows, grad_out,
             layer_input, routes, residual, both_weight, const_value, moe_gain, attn_gain,
             q2, k2, v2, o2, lse, attn_rows, qkv_weight, out_double, table):
    local, width = hidden.shape
    group = local * n_t
    ffn_count = expert_part.shape[0]
    units = expert_part.shape[-1]
    step = width // dp_count
    half = dp_count // 2
    dp_bits = log2_of(dp_count)
    inside = reduced_inside(step)
    stage_count = dp_bits - 1 if inside else 0
    tensor_bits = log2_of(n_t)
    heads = q2.shape[0]
    qkv_width = qkv_weight.shape[1]
    attn_width = qkv_width + -(-heads // 2) * 128
    attn_split = attn_width // 2 // 128 * 128
    bf, f32 = jnp.bfloat16, jnp.float32
    dma = pltpu.SemaphoreType.DMA
    rounds = dp_bits + tensor_bits

    def numbers(stage):
        return half >> (stage + 1)

    def line(rows_shape):
        return pltpu.VMEM((n_t + 1, *rows_shape[1:]), bf)

    block_shape = (n_t, local, width)
    reduction = []
    if inside:
        reduction = [
            pltpu.VMEM((1, 2, half, step, attn_width), bf),
            pltpu.VMEM((ffn_count, half, step, units), bf),
            pltpu.VMEM((ffn_count, half, step, units), bf),
            *[pltpu.VMEM((ffn_count, numbers(s), step, units), bf) for s in range(stage_count)],
            pltpu.VMEM((1, half, step, attn_width), bf),
            pltpu.VMEM((1, half, step, attn_width), bf),
            *[pltpu.VMEM((1, numbers(s), step, attn_width), bf) for s in range(stage_count)],
        ]
    scratch = [
        pltpu.VMEM((n_t - 1, ffn_count, local), f32),
        pltpu.VMEM((local, width), f32),
        line(block_shape),
        line(block_shape),
        pltpu.VMEM((2, step, units), f32),
        pltpu.VMEM(block_shape, bf),
        pltpu.VMEM(block_shape, bf),
        pltpu.VMEM((local, width), f32),
        pltpu.VMEM((local, width), f32),
        pltpu.VMEM((heads, group, 128), bf),
        pltpu.VMEM((8, group), f32),
        pltpu.VMEM((heads, group, 128), f32),
        pltpu.VMEM((heads, local, 128), f32),
        pltpu.VMEM((heads, local, 128), f32),
        pltpu.VMEM((group, qkv_width), bf),
        *reduction,
        pltpu.VMEM((rounds, 24, width), f32),
        pltpu.VMEM((8, width), f32),
        pltpu.VMEM((rounds, 8, width), f32),
        dma((n_t - 1,)),
        dma((n_t - 1,)),
        dma((2, n_t)),
        dma((n_t,)),
        dma((2, n_t, 2)),
        dma((2, n_t, 2)),
        dma((2, n_t, 2)),
        dma((2, n_t, 2)),
        dma((2, n_t, 4)),
        dma((2, n_t, 4)),
        *[
            s
            for n in ((ffn_count, 1) if inside else ())
            for s in (
                dma((n,)),
                dma((n,)),
                dma((n,)),
                *[dma((n, 2, numbers(s))) for s in range(stage_count)],
                *[dma((n, 2, numbers(s))) for s in range(stage_count)],
            )
        ],
        dma((rounds,)),
        dma((rounds,)),
        dma((rounds,)),
        dma((rounds,)),
        dma((ffn_count,)),
    ]
    vmem = pl.BlockSpec(memory_space=pltpu.VMEM)
    operands = (ffn_part, ffn_back, chosen, expert_part, hidden, moe_rows, grad_out, layer_input,
                routes, residual, both_weight, const_value, moe_gain, attn_gain, q2, k2, v2, o2,
                lse, attn_rows, qkv_weight, out_double, table)
    specs = [vmem] * len(operands)
    specs[3] = pl.BlockSpec(memory_space=pl.ANY)
    return pl.pallas_call(
        functools.partial(
            backward_kernel, (dp_bits, n_t, ffn_count, residual.shape[1], attn_split, inside)
        ),
        out_shape=(
            jax.ShapeDtypeStruct((local, width), bf),
            jax.ShapeDtypeStruct((local, width), bf),
            jax.ShapeDtypeStruct((ffn_count, step, units) if inside else (8, 128), f32),
            jax.ShapeDtypeStruct((step, attn_width), f32)
            if inside
            else jax.ShapeDtypeStruct((1, 2, half, step, attn_width), bf),
            jax.ShapeDtypeStruct((24, width), f32),
            jax.ShapeDtypeStruct((8, width), f32),
        ),
        in_specs=specs,
        out_specs=(vmem, vmem, pl.BlockSpec(memory_space=pl.ANY), vmem, vmem, vmem),
        scratch_shapes=scratch,
        compiler_params=pltpu.CompilerParams(
            collective_id=1, has_side_effects=True, vmem_limit_bytes=62 << 20
        ),
        name="backward",
    )(*operands)


def rope_lanes(length, head_width):
    position = np.arange(length, dtype=np.float64)[:, None]
    inverse = np.exp(np.arange(head_width // 2) * (-2.0 * math.log(10000.0) / head_width))
    angle = position * inverse[None, :]
    c, s = np.cos(angle), np.sin(angle)
    cosine = np.concatenate([c, c, c, c], axis=1).astype(np.float32)
    sine = np.concatenate([-s, s, s, -s], axis=1).astype(np.float32)
    return cosine, sine


def tidy_kernel(route_count, expert_ref, gate_out, up_out, down_out):
    units = gate_out.shape[2]
    gate_out[...] = expert_ref[:, :, 0:units]
    up_out[...] = expert_ref[:, :, units : 2 * units]
    down_out[0] = expert_ref[0, :, 2 * units :].T


def tidy(expert_sum):
    count, step, width = expert_sum.shape
    units = width // 3
    shape = jax.ShapeDtypeStruct((count, step, units), jnp.float32)
    spec = pl.BlockSpec((1, step, units), lambda e: (e, 0, 0))
    return pl.pallas_call(
        functools.partial(tidy_kernel, 0),
        grid=(count,),
        out_shape=(shape, shape, jax.ShapeDtypeStruct((count, units, step), jnp.float32)),
        in_specs=[pl.BlockSpec((1, step, width), lambda e: (e, 0, 0))],
        out_specs=(spec, spec, pl.BlockSpec((1, units, step), lambda e: (e, 0, 0))),
        compiler_params=pltpu.CompilerParams(dimension_semantics=("arbitrary",)),
        name="tidy",
    )(expert_sum)


def on_device(
    layer_input,
    attn_gain,
    query_weight,
    key_weight,
    value_weight,
    out_weight,
    moe_gain,
    router_weight,
    gate_residual,
    const_gate,
    const_value,
    gate_weight,
    up_weight,
    down_weight,
    routes,
    grad_out,
):
    local_rows, model_width = layer_input.shape
    tensor_size = lax.axis_size("tensor")
    group_rows = local_rows * tensor_size
    seq_count = group_rows // LENGTH
    head_count = query_weight.shape[1] // HD
    ffn_count = gate_weight.shape[0]
    route_count = router_weight.shape[1]
    cosine, sine = rope_tables(LENGTH, HD)
    input_wide = layer_input.astype(jnp.float32)
    norm_attn = rms_norm(input_wide, attn_gain)
    norm_attn = norm_attn.astype(jnp.bfloat16)
    attn_rows = lax.all_gather(norm_attn, "tensor", axis=0, tiled=True)
    query_raw = jnp.dot(attn_rows, query_weight, preferred_element_type=jnp.float32).reshape(
        seq_count, LENGTH, head_count, HD
    )
    key_raw = jnp.dot(attn_rows, key_weight, preferred_element_type=jnp.float32).reshape(
        seq_count, LENGTH, head_count, HD
    )
    value_raw = jnp.dot(attn_rows, value_weight, preferred_element_type=jnp.float32).reshape(
        seq_count, LENGTH, head_count, HD
    )
    query = rotate(query_raw, cosine, sine).astype(jnp.bfloat16)
    key = rotate(key_raw, cosine, sine).astype(jnp.bfloat16)
    value = value_raw.astype(jnp.bfloat16)
    mixed, log_totals = attention_forward(query, key, value)
    mixed_wide = mixed
    mixed = mixed.reshape(group_rows, head_count * HD).astype(jnp.bfloat16)
    attn_part = jnp.dot(mixed, out_weight, preferred_element_type=jnp.float32)
    attn_sum = lax.psum_scatter(
        attn_part.astype(jnp.bfloat16), "tensor", scatter_dimension=0, tiled=True
    ).astype(jnp.float32)
    hidden = input_wide + attn_sum
    norm_moe = rms_norm(hidden, moe_gain)
    norm_moe = norm_moe.astype(jnp.bfloat16)
    moe_rows = lax.all_gather(norm_moe, "tensor", axis=0, tiled=True)
    n_dp = lax.axis_size("dp")
    grad_rows = lax.all_gather(grad_out, "tensor", axis=0, tiled=True)
    pad = ((0, EXP_PAD - route_count), (0, 0))
    ffn_part, ffn_back, chosen_t, expert_part = experts(
        n_dp,
        tensor_size,
        route_count,
        moe_rows,
        grad_rows,
        routes.T,
        jnp.pad(gate_residual.T, pad),
        jnp.pad(router_weight.T, pad),
        gate_weight,
        up_weight,
        down_weight,
    )
    gates = jnp.transpose(const_gate, (1, 0, 2)).reshape(model_width, -1)
    both_weight = jnp.concatenate(
        [router_weight, gates, jnp.zeros((model_width, 128 - 4 - route_count), jnp.float32)], axis=1
    )

    def swap(values):
        return jnp.concatenate([values[..., 32:], values[..., :32]], axis=-1)

    def by_head(values, other):
        values = values.reshape(group_rows, head_count, HD)
        return jnp.transpose(jnp.concatenate([values, other(values)], axis=-1), (1, 0, 2))

    q2 = by_head(query, swap)
    k2 = by_head(key, swap)
    v2 = by_head(value, lambda x: x)
    o2 = by_head(mixed, lambda x: x)
    lse = jnp.transpose(log_totals, (1, 0, 2)).reshape(head_count, group_rows)
    lse = jnp.pad(lse, ((0, 8 - head_count), (0, 0)))
    qkv_weight = jnp.concatenate([query_weight, key_weight, value_weight], axis=1)
    qkv_weight = jnp.pad(qkv_weight, ((0, 0), (0, -qkv_weight.shape[1] % 128)))
    out_double = out_weight.reshape(head_count, 1, HD, model_width)
    out_double = jnp.broadcast_to(out_double, (head_count, 2, HD, model_width)).reshape(
        head_count * 2 * HD, model_width
    )
    cosine, sine = rope_lanes(LENGTH, HD)
    blocks = (tensor_size, local_rows, model_width)
    row_start = lax.axis_index("tensor") * local_rows
    local_routes = lax.dynamic_slice_in_dim(routes, row_start, local_rows, 0)
    local_residual = lax.dynamic_slice_in_dim(gate_residual, row_start, local_rows, 0)
    output, input_grad, expert_sum, attn_sum_rows, small, gain = backward(
        n_dp,
        tensor_size,
        ffn_part.reshape(blocks),
        ffn_back.reshape(blocks),
        chosen_t,
        expert_part,
        hidden,
        moe_rows.reshape(blocks),
        grad_out,
        layer_input,
        local_routes,
        local_residual,
        both_weight,
        const_value,
        moe_gain.reshape(1, model_width),
        attn_gain.reshape(1, model_width),
        q2,
        k2,
        v2,
        o2,
        lse,
        attn_rows.reshape(blocks),
        qkv_weight,
        out_double,
        jnp.asarray(np.concatenate([cosine[:, :HD], sine[:, HD:]], axis=1)),
    )
    if not reduced_inside(model_width // n_dp):

        def scattered(pairs):
            pairs = jnp.transpose(pairs, (2, 1, 3, 0, 4)).reshape(model_width, -1)
            return lax.psum_scatter(pairs, "dp", scatter_dimension=0, tiled=True).astype(
                jnp.float32
            )

        attn_sum_rows = scattered(attn_sum_rows)
        expert_sum = scattered(expert_part).reshape(
            model_width // n_dp, ffn_count, expert_part.shape[-1]
        )
        expert_sum = jnp.transpose(expert_sum, (1, 0, 2))
    gate_sum, up_sum, down_sum = tidy(expert_sum)
    wide = head_count * HD
    out_at = qkv_weight.shape[1]
    both_grad = small[8:24].T
    return (
        output,
        input_grad,
        gain[0],
        attn_sum_rows[:, :wide],
        attn_sum_rows[:, wide : 2 * wide],
        attn_sum_rows[:, 2 * wide : 3 * wide],
        attn_sum_rows[:, out_at : out_at + wide].T,
        small[0],
        both_grad[:, :route_count],
        jnp.transpose(both_grad[:, route_count : route_count + 4].reshape(model_width, 2, 2), (1, 0, 2)),
        small[1:3],
        gate_sum,
        up_sum,
        down_sum,
    )


def solution(mesh):
    in_specs = (
        P(("dp", "tensor"), None),
        P(),
        P(None, "tensor"),
        P(None, "tensor"),
        P(None, "tensor"),
        P("tensor", None),
        P(),
        P(),
        P("dp", None),
        P(),
        P(),
        P(None, None, "tensor"),
        P(None, None, "tensor"),
        P(None, "tensor", None),
        P("dp", None),
        P(("dp", "tensor"), None),
    )
    out_specs = (
        P(("dp", "tensor"), None),
        P(("dp", "tensor"), None),
        P(),
        P("dp", "tensor"),
        P("dp", "tensor"),
        P("dp", "tensor"),
        P("tensor", "dp"),
        P(),
        P(),
        P(),
        P(),
        P(None, "dp", "tensor"),
        P(None, "dp", "tensor"),
        P(None, "tensor", "dp"),
    )
    return jax.shard_map(
        on_device, mesh=mesh, in_specs=in_specs, out_specs=out_specs, check_vma=False
    )
```

time: 651 us -> 464 us (0.71)
  waiting for transfers between devices: 386 us -> 130 us
  Pallas kernels: 42.2 us -> 231 us
  blocking collectives: 43.4 us -> 0 us
  matrix products: 49.3 us -> 14.2 us
  local copies, waits for them, and re-layouts: 70.2 us -> 37 us
    reduce_scatter x6 -> x0, waiting for transfers between devices: 205 us -> none  [the longest x1 119 us: on_device(): lax.psum_scatter(expert_part, 'dp', scatter_dimension=0, tiled=True)]
    pallas_call x0 -> x2, Pallas kernels: none -> 190 us  [the longest x1 183 us: backward(): pl.pallas_call(functools.partial(backward_kernel, (dp_bits, n_t, ffn_coun...]
    psum x1 -> x0, blocking collectives: 43.4 us -> none  [on_device(): lax.psum((attn_gain_part, moe_gain_part, router_part, const_gate_part, co...]
    all_gather x1 -> x0, waiting for transfers between devices: 34.9 us -> none  [on_device(): lax.all_gather(hidden_grad.astype(jnp.bfloat16), 'tensor', axis=0, tiled=...]
    dot_general x22 -> x0, matrix products: 32.6 us -> none  [the longest x2 7.86 us: block_step(): jnp.einsum('hqk,qhd->khd', soft_probs.astype(jnp.bfloat16), grad_blk, pre...]
    dynamic_update_slice x4 -> x0, local copies, waits for them, and re-layouts: 17 us -> none  [attention_forward(): lax.map(one_block, jnp.arange(seq_count * block_count, dtype=jnp.int32))]
    transpose x3 -> x2, local copies, waits for them, and re-layouts: 19.3 us -> 2.63 us  [the longest x1 1.83 us: on_device(): attn_sum_rows[:, out_at:out_at + wide]]
    all_gather x1, waiting for transfers between devices: 33.7 us -> 20.5 us  [on_device(): grad_rows = lax.all_gather(grad_out, 'tensor', axis=0, tiled=True)]
  transfers between devices with their start and end apart: 11 -> 4, of which waited for: 10 -> 4; matrix products, arithmetic and copies ran while one was open for 8% -> 4% of each run, Pallas kernels for 0% -> 0%
where the time goes in v2:
time: 464 us; the launch traced here: 457 us
  Pallas kernels  231 us (50%)
  waiting for transfers between devices  130 us (28%)
  local copies, waits for them, and re-layouts  37 us (8%)
  other arithmetic  26.9 us (6%)
  between operations  14.4 us (3%)
  matrix products  14.2 us (3%)
    pallas_call x1, Pallas kernels, backward(): pl.pallas_call(functools.partial(backward_kernel, (dp_bits, n_t, ffn_coun...  183 us
    pallas_call x1, Pallas kernels, experts(): pl.pallas_call(functools.partial(expert_kernel, n_dp, ffn_count, route_co...  41.1 us
    all_gather x1, waiting for transfers between devices, on_device(): moe_rows = lax.all_gather(norm_moe, 'tensor', axis=0, tiled=True)  38 us
    all_gather x1, waiting for transfers between devices, on_device(): attn_rows = lax.all_gather(norm_attn, 'tensor', axis=0, tiled=True)  37.2 us
    reduce_scatter x1, waiting for transfers between devices, on_device(): lax.psum_scatter(attn_part.astype(jnp.bfloat16), 'tensor', scatter_dimens...  33.2 us
    unnamed x75, local copies, waits for them, and re-layouts  20.7 us
    all_gather x1, waiting for transfers between devices, on_device(): grad_rows = lax.all_gather(grad_out, 'tensor', axis=0, tiled=True)  20.5 us
  transfers between devices with their start and end apart: 4, of which 4 were waited for; matrix products, arithmetic and copies ran while one was open for 4% of the time, Pallas kernels for 0%

profile of v2, /device:TPU:0, one launch (start us, length us, event | category | flops | bytes accessed | tf_op | source)
XLA Modules:
  0.0 457.2 jit_solution(14857060684623171608)
XLA Ops:
  7.2 1.2 fusion.24
  8.4 1.9 fusion.26
  10.4 2.7 fusion.28
  13.1 37.2 %all-gather.4.cloned.1.call-done = bf16[1024,768]{1,0:T(8,128)(2,1)} async-done(((bf16[256,768]{1,0:T(8,128)(2,1)}), bf16[1024,768]{1,0:T(8,128)(2,1)}) %all-gather.4.cloned.1.call-update) | async-done | bytes 1572880 | tf_op jit(solution)/shard_map/all_gather | solution.py:1140
  50.3 2.2 fusion.32
  52.6 0.7 fusion.31
  53.3 0.8 fusion.30
  54.1 2.6 copy.63
  56.7 1.6 copy.65
  58.3 1.6 copy.62
  60.0 1.6 copy.64
  61.6 3.8 subtract_convert_fusion
  65.4 2.0 pad_maximum_fusion
  67.4 1.4 copy.47
  68.8 1.4 copy.48
  70.3 2.4 convolution_convert_fusion.1
  72.7 16.8 %while.15 = (s32[]{:T(128)}, bf16[2,512,3,64]{1,3,2,0:T(8,128)(2,1)S(1)}, f32[2,3,512]{2,1,0:T(4,128)S(1)}, s32[2]{0:T(128)S(1)}, bf16[1,1024,3,64]{1,3,2,0:T(8,...) while((s32[]{:T(128)}, ...), condition=%wide.region_4.5_spmd, body=%wide.region_1.4_spmd.sunk | while | flops 422066688 | bytes 23992656 | solution.py:99
  72.7 0.6 dynamic_slice.36
  75.6 1.4 fusion.46
  77.0 1.8 fusion.47
  78.8 2.2 fusion.48
  81.1 0.6 dynamic_slice.36
  84.0 1.4 fusion.46
  85.4 1.8 fusion.47
  87.2 2.2 fusion.48
  89.5 0.4 copy.49
  89.9 0.5 copy-done.15
  90.4 1.8 convolution_convert_fusion
  92.3 0.7 all-gather.8.cloned.1.call-update
  93.3 33.2 %reduce-scatter.2.cloned.1.call-done = bf16[256,768]{1,0:T(8,128)(2,1)} async-done(((bf16[1024,768]{1,0:T(8,128)(2,1)}), bf16[256,768]{1,0:T(8,128)(2,1)}) %reduce-scatter.2.cloned.1.call-update) | async-done | bytes 393232 | tf_op jit(solution)/shard_map/reduce_scatter | solution.py:1157
  126.5 2.1 convert_add_fusion
  128.7 0.9 multiply_convert_fusion
  129.6 0.6 broadcast_in_dim.66.attn_gain_ref
  130.2 0.6 broadcast_in_dim.65.moe_gain_ref
  131.1 1.1 copy.59
  132.6 0.8 copy.67.residual_ref
  133.3 0.8 copy.66.routes_ref
  134.4 1.3 fusion.23.qkv_ref
  135.7 0.9 maximum_maximum_fusion.both_ref
  137.0 0.4 copy.54
  137.4 0.6 pad.18.lse_ref
  138.1 1.3 maximum_bitcast_fusion.2.v_ref
  139.4 1.3 maximum_bitcast_fusion.3.o_ref
  140.7 3.0 maximum_bitcast_fusion
  143.7 20.5 %all-gather.8.cloned.1.call-done.grad_ref = bf16[1024,768]{1,0:T(8,128)(2,1)} async-done(((bf16[256,768]{1,0:T(8,128)(2,1)}), bf16[1024,768]{1,0:T(8,128)(2,1)}) %all-gather.8.cloned.1.call-update) | async-done | bytes 1572880 | tf_op jit(solution)/shard_map/all_gather | solution.py:1165
  164.2 38.0 %all-gather.6.cloned.1.call-done.moe_ref = bf16[1024,768]{1,0:T(8,128)(2,1)} async-done(((bf16[256,768]{1,0:T(8,128)(2,1)}), bf16[1024,768]{1,0:T(8,128)(2,1)}) %all-gather.6.cloned.1.call-update) | async-done | bytes 1572880 | tf_op jit(solution)/shard_map/all_gather | solution.py:1163
  202.2 1.4 copy-done
  203.6 41.1 %experts.1 = (bf16[1024,768]{1,0:T(8,128)(2,1)S(1)}, bf16[1024,768]{1,0:T(8,128)(2,1)S(1)}, f32[4,8,256]{2,1,0:T(8,128)S(1)}, bf16[8,2,4,96,1536]{4,3,2,1,0:T(8,128)(2,1)}) custom-call(bf16[1024,768]{1,0:T(8,128)(2,1)S(1)} %copy-done, bf16[1024,768]{1,0:T(8,128)(2,1)} %all-gather.8.cloned.1.call-done.grad_ref, s32[2,1024]{1,0:T(2,128)S(1)} %bitcast.90, ...), custom_call_target="tpu_custom_call" | custom-call | tf_op jit(solution)/shard_map/experts/pallas_call | solution.py:232
  244.7 1.1 copy-done.1
  245.8 1.1 copy-done.2
  247.0 0.6 copy-done.3
  247.6 0.9 broadcast_in_dim.68
  248.5 182.6 %backward.1 = (bf16[256,768]{1,0:T(8,128)(2,1)}, bf16[256,768]{1,0:T(8,128)(2,1)}, f32[8,96,1536]{2,1,0:T(8,128)}, f32[96,896]{1,0:T(8,128)}, f32[24,768]{1,0:T(8,128)}, /*index=5*/f32[8,768]{1,0:T(8,128)}) custom-call(bf16[4,256,768]{2,1,0:T(8,128)(2,1)} %bitcast.88, bf16[4,256,768]{2,1,0:T(8,128)(2,1)} %bitcast.89, f32[4,8,256]{2,1,0:T(8,128)} %copy-done.3, ...), custom_call_target="tpu_custom_call" | custom-call | tf_op jit(solution)/shard_map/backward/pallas_call | solution.py:1054
  431.0 1.3 slice_reduce_fusion
  432.4 1.3 slice.59
  433.7 0.8 slice_bitcast_fusion.1
  434.5 1.4 slice_reduce_fusion.1
  435.9 0.6 reshape.323
  436.5 1.8 slice_bitcast_fusion
  438.3 0.7 copy.60
  439.1 7.0 %tidy.1 = (f32[8,96,512]{2,1,0:T(8,128)}, f32[8,96,512]{2,1,0:T(8,128)}, f32[8,512,96]{2,1,0:T(8,128)}) custom-call(f32[8,96,1536]{2,1,0:T(8,128)} %get-tuple-element.157.expert_ref), custom_call_target="tpu_custom_call" | custom-call | tf_op jit(solution)/shard_map/tidy/pallas_call | solution.py:1100
  446.1 2.8 copy.61
  449.0 0.7 copy.82
  449.7 0.7 copy.83
  (95 shorter events, 2.7 us)
Async XLA Ops:
  7.2 43.1 %copy-start.19 = (bf16[768,192]{0,1:T(8,128)(2,1)S(1)}, bf16[768,192]{0,1:T(8,128)(2,1)}, u32[]{:S(2)}) copy-start(bf16[768,192]{0,1:T(8,128)(2,1)} %param.22) | copy-start | bytes 884740
  7.2 43.1 %all-gather.4.cloned.1.call-start = ((), (), s32[]{:S(2)}) async-start(), calls=%async_computation.1 | async-start | bytes 1966080 | tf_op jit(solution)/shard_map/all_gather | solution.py:1140
  10.4 116.2 %reduce-scatter.2.cloned.1.call-start = ((), (), s32[]{:S(2)}) async-start(), calls=%async_computation.2 | async-start | bytes 1966080 | tf_op jit(solution)/shard_map/reduce_scatter | solution.py:1157
  13.1 39.4 %copy-start.17 = (bf16[768,192]{0,1:T(8,128)(2,1)S(1)}, bf16[768,192]{0,1:T(8,128)(2,1)}, u32[]{:S(2)}) copy-start(bf16[768,192]{0,1:T(8,128)(2,1)} %param.21) | copy-start | bytes 884740
  50.3 2.3 copy-start.5
  65.4 2.0 copy-start.7
  65.4 2.0 copy-start.9
  65.4 2.0 copy-start.11
  68.8 3.8 copy-start.13
  77.0 1.8 copy-start.23
  85.4 1.8 copy-start.23
  89.4 1.0 copy-start.15
  90.4 36.1 %copy-start.6 = (bf16[256,768]{1,0:T(8,128)(2,1)S(1)}, bf16[256,768]{1,0:T(8,128)(2,1)}, u32[]{:S(2)}) copy-start(bf16[256,768]{1,0:T(8,128)(2,1)} %input_ref.1) | copy-start | bytes 1179652
  92.2 36.4 %copy-start.29 = (f32[768]{0:T(1024)S(1)}, f32[768]{0:T(1024)}, u32[]{:S(2)}) copy-start(f32[768]{0:T(1024)} %param.25) | copy-start | bytes 9220
  92.2 72.0 %all-gather.8.cloned.1.call-start = ((), (), s32[]{:S(2)}) async-start(), calls=%async_computation.4 | async-start | bytes 1966080 | tf_op jit(solution)/shard_map/all_gather | solution.py:1165
  92.9 36.7 %copy-start.28 = (f32[768]{0:T(1024)S(1)}, f32[768]{0:T(1024)}, u32[]{:S(2)}) copy-start(f32[768]{0:T(1024)} %param.20) | copy-start | bytes 9220
  93.0 37.8 %copy-start.18 = (bf16[768,192]{0,1:T(8,128)(2,1)S(1)}, bf16[768,192]{0,1:T(8,128)(2,1)}, u32[]{:S(2)}) copy-start(bf16[768,192]{0,1:T(8,128)(2,1)} %param.21) | copy-start | bytes 884740
  93.0 38.0 %copy-start.20 = (bf16[768,192]{0,1:T(8,128)(2,1)S(1)}, bf16[768,192]{0,1:T(8,128)(2,1)}, u32[]{:S(2)}) copy-start(bf16[768,192]{0,1:T(8,128)(2,1)} %param.22) | copy-start | bytes 884740
  93.0 109.2 %all-gather.6.cloned.1.call-start = ((), (), s32[]{:S(2)}) async-start(), calls=%async_computation.3 | async-start | bytes 1966080 | tf_op jit(solution)/shard_map/all_gather | solution.py:1163
  126.5 2.1 copy-start.14
  128.6 3.6 copy-start.30
  128.6 3.7 copy-start.25
  129.6 3.0 copy-start.26
  129.6 3.7 copy-start.4
  135.7 1.3 copy-start.24
  138.1 2.6 copy-start.8
  138.1 2.6 copy-start.10
  138.1 2.6 copy-start.12
  202.2 1.4 copy-start
  203.6 44.0 %copy-start.16 = (bf16[192,768]{1,0:T(8,128)(2,1)S(1)}, bf16[192,768]{1,0:T(8,128)(2,1)}, u32[]{:S(2)}) copy-start(bf16[192,768]{1,0:T(8,128)(2,1)} %param.24) | copy-start | bytes 884740
  244.7 1.1 copy-start.1
  245.8 1.1 copy-start.2
  247.0 0.6 copy-start.3
  434.5 11.6 %copy-start.27 = (f32[768,16]{0,1:T(8,128)}, f32[768,16]{0,1:T(8,128)S(1)}, u32[]{:S(2)}) copy-start(f32[768,16]{0,1:T(8,128)S(1)} %slice_bitcast_fusion.1) | copy-start | bytes 147460
  446.1 2.9 copy-start.22
  446.1 3.6 copy-start.21
Sparse Core Ops, SparseCore 0:
  10.5 39.7 all-gather.3
  92.3 34.1 reduce-scatter.1
  128.1 36.0 all-gather.7
  166.2 35.9 all-gather.5

commit v3 on v2

--- a/solution.py
+++ b/solution.py
@@ -17,86 +17,6 @@
 
 EPSILON = 1e-06
 MASKED = -1e30
-
-
-def rope_tables(length, head_width):
-    position = jnp.arange(length, dtype=jnp.float32)[:, None]
-    inverse = jnp.exp(
-        jnp.arange(head_width // 2, dtype=jnp.float32) * (-2.0 * math.log(10000.0) / head_width)
-    )
-    angle = position * inverse[None, :]
-    return (jnp.cos(angle), jnp.sin(angle))
-
-
-def rotate(values, cosine, sine):
-    half_width = values.shape[-1] // 2
-    first_half = values[..., :half_width]
-    second_half = values[..., half_width:]
-    cos_table = cosine[:, None, :]
-    sin_table = sine[:, None, :]
-    return jnp.concatenate(
-        [
-            first_half * cos_table - second_half * sin_table,
-            second_half * cos_table + first_half * sin_table,
-        ],
-        axis=-1,
-    )
-
-
-def unrotate(values, cosine, sine):
-    half_width = values.shape[-1] // 2
-    first_half = values[..., :half_width]
-    second_half = values[..., half_width:]
-    cos_table = cosine[:, None, :]
-    sin_table = sine[:, None, :]
-    return jnp.concatenate(
-        [
-            first_half * cos_table + second_half * sin_table,
-            second_half * cos_table - first_half * sin_table,
-        ],
-        axis=-1,
-    )
-
-
-def rms_norm(values, gain):
-    scale = lax.rsqrt(jnp.mean(values * values, axis=-1, keepdims=True) + EPSILON)
-    return values * scale * gain
-
-
-def block_mask(query_start, query_rows, length):
-    query_pos = query_start + jnp.arange(query_rows, dtype=jnp.int32)
-    key_pos = jnp.arange(length, dtype=jnp.int32)
-    return (key_pos // BLOCK)[None, :] <= (query_pos // BLOCK)[:, None]
-
-
-def attention_forward(query, key, value):
-    seq_count, length, head_count, head_width = query.shape
-    query_rows = min(512, length)
-    block_count = length // query_rows
-    scale = head_width ** (-0.5)
-
-    def one_block(block_index):
-        seq_index = block_index // block_count
-        query_start = block_index % block_count * query_rows
-        query_seq = lax.dynamic_index_in_dim(query, seq_index, 0, keepdims=False)
-        query_blk = lax.dynamic_slice_in_dim(query_seq, query_start, query_rows, 0)
-        key_seq = lax.dynamic_index_in_dim(key, seq_index, 0, keepdims=False)
-        value_seq = lax.dynamic_index_in_dim(value, seq_index, 0, keepdims=False)
-        scores = (
-            jnp.einsum("qhd,khd->hqk", query_blk, key_seq, preferred_element_type=jnp.float32)
-            * scale
-        )
-        scores = jnp.where(block_mask(query_start, query_rows, length)[None], scores, MASKED)
-        row_max = jnp.max(scores, axis=-1, keepdims=True)
-        exp_scores = jnp.exp(scores - row_max)
-        row_total = jnp.sum(exp_scores, axis=-1, keepdims=True)
-        soft_probs = (exp_scores / row_total).astype(jnp.bfloat16)
-        result = jnp.einsum(
-            "hqk,khd->qhd", soft_probs, value_seq, preferred_element_type=jnp.float32
-        )
-        return (result, (row_max + jnp.log(row_total))[..., 0])
-
-    return lax.map(one_block, jnp.arange(seq_count * block_count, dtype=jnp.int32))
 
 
 EXP_PAD = 16
@@ -558,6 +478,203 @@
     def take(self, n):
         self.copy(n).wait()
         self.total[...] += self.arrived[n]
+
+
+def select_lanes(rows, columns, source):
+    row = lax.broadcasted_iota(jnp.int32, (rows, columns), 0)
+    column = lax.broadcasted_iota(jnp.int32, (rows, columns), 1)
+    return jnp.where(row == source(column), 1.0, 0.0).astype(jnp.bfloat16)
+
+
+def forward_kernel(
+    n_t,
+    input_ref,
+    attn_gain_ref,
+    moe_gain_ref,
+    q_w_ref,
+    k_w_ref,
+    v_w_ref,
+    out_w_ref,
+    grad_ref,
+    cos_ref,
+    sin_ref,
+    q_out,
+    k_out,
+    v_out,
+    o_out,
+    lse_out,
+    rows_out,
+    moe_out,
+    grad_out,
+    hidden_out,
+    qkv_out,
+    double_out,
+    weights,
+    part,
+    arrived,
+    acc,
+    rows_send,
+    rows_recv,
+    grad_send,
+    grad_recv,
+    moe_send,
+    moe_recv,
+    line_send,
+    line_recv,
+):
+    place = lax.axis_index("tensor")
+    heads = q_out.shape[0]
+    local, width = input_ref.shape
+    barrier = pltpu.get_barrier_semaphore()
+    for step in range(1, n_t):
+        pl.semaphore_signal(
+            barrier,
+            inc=1,
+            device_id={"tensor": (place + step) % n_t},
+            device_id_type=MESH,
+        )
+    wide = input_ref[...].astype(jnp.float32)
+    scale = lax.rsqrt(jnp.mean(wide * wide, axis=1, keepdims=True) + EPSILON)
+    rows_out[place] = (wide * scale * attn_gain_ref[...]).astype(jnp.bfloat16)
+    grad_out[place] = grad_ref[...]
+    pl.semaphore_wait(barrier, n_t - 1)
+
+    rows_gather = LineGather(rows_out, rows_send, rows_recv, place)
+    grad_gather = LineGather(grad_out, grad_send, grad_recv, place)
+    moe_gather = LineGather(moe_out, moe_send, moe_recv, place)
+    line = LineScatter(part, arrived, line_send, line_recv, place, 4)
+    rows_gather.start()
+
+    columns = heads * HD
+    twice = select_lanes(columns, heads * 128, lambda c: c // 128 * HD + c % HD)
+    swapped = select_lanes(
+        columns,
+        heads * 128,
+        lambda c: c // 128 * HD + (c % HD + c % 128 // HD * (HD // 2)) % HD,
+    )
+    for n, (ref, lanes) in enumerate(
+        ((q_w_ref, swapped), (k_w_ref, swapped), (v_w_ref, twice))
+    ):
+        weights[:, n * heads * 128 : (n + 1) * heads * 128] = dot(ref[...], lanes).astype(
+            jnp.bfloat16
+        )
+    joined = jnp.zeros(qkv_out.shape, jnp.float32)
+    for n, ref in enumerate((q_w_ref, k_w_ref, v_w_ref)):
+        lanes = select_lanes(columns, qkv_out.shape[1], lambda c, n=n: c - n * columns)
+        joined = joined + dot(ref[...], lanes)
+    qkv_out[...] = joined.astype(jnp.bfloat16)
+    double_out[...] = dot_tn(twice, out_w_ref[...]).astype(jnp.bfloat16)
+
+    def project(block):
+        at = pl.ds(pl.multiple_of(block * local, local), local)
+        product = dot(rows_out[block], weights[...])
+        cosine, sine = cos_ref[at, :], sin_ref[at, :]
+        for n, target in enumerate((q_out, k_out, v_out)):
+            for h in range(heads):
+                start = (n * heads + h) * 128
+                piece = product[:, start : start + 128]
+                if n < 2:
+                    piece = piece * cosine + pltpu.roll(piece, 64, 1) * sine
+                target[h, at, :] = piece.astype(jnp.bfloat16)
+
+    def arrive(distance, _):
+        @pl.when(distance > 0)
+        def _():
+            rows_gather.step(distance)
+
+        def side(way, _):
+            block = place + (2 * way - 1) * distance
+
+            @pl.when((block >= 0) & (block < n_t) & ((distance > 0) | (way == 0)))
+            def _():
+                project(block)
+
+            return 0
+
+        lax.fori_loop(0, 2, side, 0)
+        return 0
+
+    lax.fori_loop(0, n_t, arrive, 0)
+    grad_gather.start()
+
+    factor = 0.5 * HD ** (-0.5)
+
+    lse_out[...] = jnp.zeros_like(lse_out)
+
+    def attend(block):
+        at = slice(block * local, (block + 1) * local)
+        seen = (block + 1) * local
+        mixed = []
+        for h in range(heads):
+            scores = dot_nt(q_out[h, at, :], k_out[h, 0:seen, :]) * factor
+            top = jnp.max(scores, axis=1, keepdims=True)
+            exps = jnp.exp(scores - top)
+            total = jnp.sum(exps, axis=1, keepdims=True)
+            probs = (exps / total).astype(jnp.bfloat16)
+            out = dot(probs, v_out[h, 0:seen, :]).astype(jnp.bfloat16)
+            o_out[h, at, :] = out
+            mixed.append(out)
+            log_total = jnp.broadcast_to(top + jnp.log(total), (local, 128))
+            lse_out[h : h + 1, at] = log_total.T[0:1, :]
+        mixed = jnp.concatenate(mixed, axis=1)
+        part[block] = (0.5 * dot(mixed, double_out[...])).astype(jnp.bfloat16)
+
+    order = (*range(1, n_t), 0)
+    for n, block in enumerate(order):
+        attend(block)
+        line.originate(block)
+        if n > 0:
+            grad_gather.step(n)
+            line.forward(order[n - 1])
+    line.forward(order[-1])
+    line.collect(acc)
+    hidden = input_ref[...].astype(jnp.float32) + acc[...]
+    hidden_out[...] = hidden
+    scale = lax.rsqrt(jnp.mean(hidden * hidden, axis=1, keepdims=True) + EPSILON)
+    moe_out[place] = (hidden * scale * moe_gain_ref[...]).astype(jnp.bfloat16)
+    moe_gather.start()
+    for step in range(1, n_t):
+        moe_gather.step(step)
+    for exchange in (rows_gather, grad_gather, moe_gather, line):
+        exchange.finish()
+
+
+def forward(n_t, layer_input, attn_gain, moe_gain, q_w, k_w, v_w, out_w, grad_out, cosine, sine):
+    local, width = layer_input.shape
+    group = local * n_t
+    heads = q_w.shape[1] // HD
+    bf, f32 = jnp.bfloat16, jnp.float32
+    dma = pltpu.SemaphoreType.DMA
+    vmem = pl.BlockSpec(memory_space=pltpu.VMEM)
+    blocks = (n_t, local, width)
+    qkv_width = -(-3 * heads * HD // 128) * 128
+    outs = (
+        *[jax.ShapeDtypeStruct((heads, group, 128), bf)] * 4,
+        jax.ShapeDtypeStruct((8, group), f32),
+        *[jax.ShapeDtypeStruct(blocks, bf)] * 3,
+        jax.ShapeDtypeStruct((local, width), f32),
+        jax.ShapeDtypeStruct((width, qkv_width), bf),
+        jax.ShapeDtypeStruct((heads * 128, width), bf),
+    )
+    return pl.pallas_call(
+        functools.partial(forward_kernel, n_t),
+        out_shape=outs,
+        in_specs=[vmem] * 10,
+        out_specs=(vmem,) * len(outs),
+        scratch_shapes=[
+            pltpu.VMEM((width, 3 * heads * 128), bf),
+            pltpu.VMEM(blocks, bf),
+            pltpu.VMEM((n_t + 1, local, width), bf),
+            pltpu.VMEM((local, width), f32),
+            *[s for _ in range(3) for s in (dma((2, n_t)), dma((n_t,)))],
+            dma((2, n_t, 4)),
+            dma((2, n_t, 4)),
+        ],
+        compiler_params=pltpu.CompilerParams(
+            collective_id=2, has_side_effects=True, vmem_limit_bytes=56 << 20
+        ),
+        name="forward",
+    )(layer_input, attn_gain, moe_gain, q_w, k_w, v_w, out_w, grad_out, cosine, sine)
 
 
 def side_forward(norm, named, residual, weight_parts, const_value, route_count, ffn_count):
@@ -1129,47 +1246,33 @@
     local_rows, model_width = layer_input.shape
     tensor_size = lax.axis_size("tensor")
     group_rows = local_rows * tensor_size
-    seq_count = group_rows // LENGTH
     head_count = query_weight.shape[1] // HD
     ffn_count = gate_weight.shape[0]
     route_count = router_weight.shape[1]
-    cosine, sine = rope_tables(LENGTH, HD)
-    input_wide = layer_input.astype(jnp.float32)
-    norm_attn = rms_norm(input_wide, attn_gain)
-    norm_attn = norm_attn.astype(jnp.bfloat16)
-    attn_rows = lax.all_gather(norm_attn, "tensor", axis=0, tiled=True)
-    query_raw = jnp.dot(attn_rows, query_weight, preferred_element_type=jnp.float32).reshape(
-        seq_count, LENGTH, head_count, HD
-    )
-    key_raw = jnp.dot(attn_rows, key_weight, preferred_element_type=jnp.float32).reshape(
-        seq_count, LENGTH, head_count, HD
-    )
-    value_raw = jnp.dot(attn_rows, value_weight, preferred_element_type=jnp.float32).reshape(
-        seq_count, LENGTH, head_count, HD
-    )
-    query = rotate(query_raw, cosine, sine).astype(jnp.bfloat16)
-    key = rotate(key_raw, cosine, sine).astype(jnp.bfloat16)
-    value = value_raw.astype(jnp.bfloat16)
-    mixed, log_totals = attention_forward(query, key, value)
-    mixed_wide = mixed
-    mixed = mixed.reshape(group_rows, head_count * HD).astype(jnp.bfloat16)
-    attn_part = jnp.dot(mixed, out_weight, preferred_element_type=jnp.float32)
-    attn_sum = lax.psum_scatter(
-        attn_part.astype(jnp.bfloat16), "tensor", scatter_dimension=0, tiled=True
-    ).astype(jnp.float32)
-    hidden = input_wide + attn_sum
-    norm_moe = rms_norm(hidden, moe_gain)
-    norm_moe = norm_moe.astype(jnp.bfloat16)
-    moe_rows = lax.all_gather(norm_moe, "tensor", axis=0, tiled=True)
+    attn_gain_row = attn_gain.reshape(1, model_width)
+    moe_gain_row = moe_gain.reshape(1, model_width)
+    cosine, sine = rope_lanes(LENGTH, HD)
+    q2, k2, v2, o2, lse, attn_rows, moe_rows, grad_rows, hidden, qkv_weight, out_double = forward(
+        tensor_size,
+        layer_input,
+        attn_gain_row,
+        moe_gain_row,
+        query_weight,
+        key_weight,
+        value_weight,
+        out_weight,
+        grad_out,
+        jnp.asarray(cosine),
+        jnp.asarray(sine),
+    )
     n_dp = lax.axis_size("dp")
-    grad_rows = lax.all_gather(grad_out, "tensor", axis=0, tiled=True)
     pad = ((0, EXP_PAD - route_count), (0, 0))
     ffn_part, ffn_back, chosen_t, expert_part = experts(
         n_dp,
         tensor_size,
         route_count,
-        moe_rows,
-        grad_rows,
+        moe_rows.reshape(group_rows, model_width),
+        grad_rows.reshape(group_rows, model_width),
         routes.T,
         jnp.pad(gate_residual.T, pad),
         jnp.pad(router_weight.T, pad),
@@ -1182,26 +1285,6 @@
         [router_weight, gates, jnp.zeros((model_width, 128 - 4 - route_count), jnp.float32)], axis=1
     )
 
-    def swap(values):
-        return jnp.concatenate([values[..., 32:], values[..., :32]], axis=-1)
-
-    def by_head(values, other):
-        values = values.reshape(group_rows, head_count, HD)
-        return jnp.transpose(jnp.concatenate([values, other(values)], axis=-1), (1, 0, 2))
-
-    q2 = by_head(query, swap)
-    k2 = by_head(key, swap)
-    v2 = by_head(value, lambda x: x)
-    o2 = by_head(mixed, lambda x: x)
-    lse = jnp.transpose(log_totals, (1, 0, 2)).reshape(head_count, group_rows)
-    lse = jnp.pad(lse, ((0, 8 - head_count), (0, 0)))
-    qkv_weight = jnp.concatenate([query_weight, key_weight, value_weight], axis=1)
-    qkv_weight = jnp.pad(qkv_weight, ((0, 0), (0, -qkv_weight.shape[1] % 128)))
-    out_double = out_weight.reshape(head_count, 1, HD, model_width)
-    out_double = jnp.broadcast_to(out_double, (head_count, 2, HD, model_width)).reshape(
-        head_count * 2 * HD, model_width
-    )
-    cosine, sine = rope_lanes(LENGTH, HD)
     blocks = (tensor_size, local_rows, model_width)
     row_start = lax.axis_index("tensor") * local_rows
     local_routes = lax.dynamic_slice_in_dim(routes, row_start, local_rows, 0)
@@ -1214,21 +1297,21 @@
         chosen_t,
         expert_part,
         hidden,
-        moe_rows.reshape(blocks),
+        moe_rows,
         grad_out,
         layer_input,
         local_routes,
         local_residual,
         both_weight,
         const_value,
-        moe_gain.reshape(1, model_width),
-        attn_gain.reshape(1, model_width),
+        moe_gain_row,
+        attn_gain_row,
         q2,
         k2,
         v2,
         o2,
         lse,
-        attn_rows.reshape(blocks),
+        attn_rows,
         qkv_weight,
         out_double,
         jnp.asarray(np.concatenate([cosine[:, :HD], sine[:, HD:]], axis=1)),

time: 464 us -> 368 us (0.79); the launches traced: 457 us -> 367 us
  waiting for transfers between devices: 130 us -> 0 us
  Pallas kernels: 231 us -> 338 us
  other arithmetic: 26.9 us -> 0.93 us
  matrix products: 14.2 us -> 0 us
  between operations: 14.4 us -> 0.75 us
  local copies, waits for them, and re-layouts: 37 us -> 27.5 us
    pallas_call x0 -> x1, Pallas kernels: none -> 112 us  [forward(): pl.pallas_call(functools.partial(forward_kernel, n_t), out_shape=outs, in...]
    all_gather x3 -> x0, waiting for transfers between devices: 95.7 us -> none  [the longest x1 38 us: on_device(): moe_rows = lax.all_gather(norm_moe, 'tensor', axis=0, tiled=True)]
    reduce_scatter x1 -> x0, waiting for transfers between devices: 33.2 us -> none  [on_device(): lax.psum_scatter(attn_part.astype(jnp.bfloat16), 'tensor', scatter_dimens...]
    dot_general x8 -> x0, matrix products: 14.2 us -> none  [the longest x2 4.4 us: one_block(): jnp.einsum('hqk,khd->qhd', soft_probs, value_seq, preferred_element_type=...]
    unnamed x75 -> x32, local copies, waits for them, and re-layouts: 20.7 us -> 14.9 us
    transpose x3 -> x0, other arithmetic: 5.62 us -> none  [by_head(): jnp.transpose(jnp.concatenate([values, other(values)], axis=-1), (1, 0, 2))]
    pallas_call x1, Pallas kernels: 183 us -> 178 us  [backward(): pl.pallas_call(functools.partial(backward_kernel, (dp_bits, n_t, ffn_coun...]
    reduce_sum x3 -> x0, other arithmetic: 4.8 us -> none  [the longest x2 3.61 us: one_block(): row_total = jnp.sum(exp_scores, axis=-1, keepdims=True)]
  transfers between devices with their start and end apart: 4 -> 0, of which waited for: 4 -> 0; matrix products, arithmetic and copies ran while one was open for 4% -> 0% of each run, Pallas kernels for 0% -> 0%
where the time goes in v3:
time: 368 us; the launch traced here: 367 us
  Pallas kernels  338 us (92%)
  local copies, waits for them, and re-layouts  27.5 us (7%)
    pallas_call x1, Pallas kernels, backward(): pl.pallas_call(functools.partial(backward_kernel, (dp_bits, n_t, ffn_coun...  178 us
    pallas_call x1, Pallas kernels, forward(): pl.pallas_call(functools.partial(forward_kernel, n_t), out_shape=outs, in...  112 us
    pallas_call x1, Pallas kernels, experts(): pl.pallas_call(functools.partial(expert_kernel, n_dp, ffn_count, route_co...  41 us
    unnamed x32, local copies, waits for them, and re-layouts  14.9 us

profile of v3, /device:TPU:0, one launch (start us, length us, event | category | flops | bytes accessed | tf_op | source)
XLA Modules:
  0.0 366.9 jit_solution(17726315287022105044)
XLA Ops:
  0.6 0.0 copy-start.9
  0.7 0.0 copy-start.8
  0.7 0.0 copy-start.7
  0.7 0.1 pad.12.clone
  0.8 0.7 constant_dynamic-slice_fusion.1
  1.5 1.3 reshape.52.attn_gain_ref
  2.8 1.3 reshape.53.moe_gain_ref
  4.0 0.7 reshape.58
  4.8 0.7 constant_dynamic-slice_fusion
  5.5 0.8 pad.9.router_ref
  6.3 0.8 pad.8.residual_ref
  7.1 0.8 copy.52.residual_ref
  7.9 0.8 copy.51.routes_ref
  8.7 0.2 copy.48
  8.9 1.9 copy.42.q_w_ref
  10.8 0.0 copy-done.7
  10.8 0.9 copy.43.k_w_ref
  11.7 0.0 copy-done.8
  11.7 0.9 copy.44.v_w_ref
  12.6 0.0 copy-done.9
  12.6 0.2 copy.47
  12.8 0.9 maximum_maximum_fusion.both_ref
  13.7 0.0 copy-start.4
  13.7 111.9 %forward.1 = (bf16[3,1024,128]{2,1,0:T(8,128)(2,1)}, bf16[3,1024,128]{2,1,0:T(8,128)(2,1)}, bf16[3,1024,128]{2,1,0:T(8,128)(2,1)}, bf16[3,1024,128]{2,1,0:T(8,12...) custom-call(bf16[256,768]{1,0:T(8,128)(2,1)} %input_ref.3, ...), custom_call_target="tpu_custom_call" | custom-call | tf_op jit(solution)/shard_map/forward/pallas_call | solution.py:659
  125.7 0.0 copy-done.4
  125.7 0.0 copy-start
  125.7 1.4 copy-done
  127.1 41.0 %experts.1 = (bf16[1024,768]{1,0:T(8,128)(2,1)S(1)}, bf16[1024,768]{1,0:T(8,128)(2,1)S(1)}, f32[4,8,256]{2,1,0:T(8,128)S(1)}, bf16[8,2,4,96,1536]{4,3,2,1,0:T(8,128)(2,1)}) custom-call(bf16[1024,768]{1,0:T(8,128)(2,1)S(1)} %bitcast.18, bf16[1024,768]{1,0:T(8,128)(2,1)} %bitcast.22, s32[2,1024]{1,0:T(2,128)S(1)} %bitcast.21, f32[16,1024]{1,0:T(8,128)S(1)} %pad.8.residual_ref, ...), custom_call_target="tpu_custom_call" | custom-call | tf_op jit(solution)/shard_map/experts/pallas_call | solution.py:152
  168.1 0.0 copy-start.1
  168.1 1.1 copy-done.1
  169.3 0.0 copy-start.2
  169.3 1.1 copy-done.2
  170.4 0.0 copy-start.3
  170.4 0.6 copy-done.3
  171.0 177.7 %backward.1 = (bf16[256,768]{1,0:T(8,128)(2,1)}, bf16[256,768]{1,0:T(8,128)(2,1)}, f32[8,96,1536]{2,1,0:T(8,128)}, f32[96,896]{1,0:T(8,128)}, f32[24,768]{1,0:T(8,128)}, /*index=5*/f32[8,768]{1,0:T(8,128)}) custom-call(bf16[4,256,768]{2,1,0:T(8,128)(2,1)} %bitcast.19, bf16[4,256,768]{2,1,0:T(8,128)(2,1)} %bitcast.20, f32[4,8,256]{2,1,0:T(8,128)} %copy-done.3, ...), custom_call_target="tpu_custom_call" | custom-call | tf_op jit(solution)/shard_map/backward/pallas_call | solution.py:1171
  348.8 1.3 slice.39
  350.1 1.4 slice_reduce_fusion
  351.5 0.8 slice_bitcast_fusion.1
  352.3 0.0 copy-start.10
  352.3 0.6 reshape.59
  352.9 1.8 slice_bitcast_fusion
  354.8 0.7 copy.49
  355.5 7.0 %tidy.1 = (f32[8,96,512]{2,1,0:T(8,128)}, f32[8,96,512]{2,1,0:T(8,128)}, f32[8,512,96]{2,1,0:T(8,128)}) custom-call(f32[8,96,1536]{2,1,0:T(8,128)} %get-tuple-element.58.expert_ref), custom_call_target="tpu_custom_call" | custom-call | tf_op jit(solution)/shard_map/tidy/pallas_call | solution.py:1217
  362.5 0.0 copy-done.10
  362.5 0.0 copy-start.6
  362.5 0.0 copy-start.5
  362.5 2.8 copy.50
  365.4 0.0 copy-done.6
  365.4 0.7 copy.55
  366.1 0.0 copy-done.5
  366.1 0.7 copy.56
  (2 shorter events, 0.0 us)
Async XLA Ops:
  0.6 12.0 %copy-start.9 = (f32[768,12]{0,1:T(8,128)S(1)}, f32[768,12]{0,1:T(8,128)}, u32[]{:S(2)}) copy-start(f32[768,12]{0,1:T(8,128)} %param.26) | copy-start | bytes 110596
  0.7 11.0 %copy-start.8 = (bf16[768,192]{0,1:T(8,128)(2,1)S(1)}, bf16[768,192]{0,1:T(8,128)(2,1)}, u32[]{:S(2)}) copy-start(bf16[768,192]{0,1:T(8,128)(2,1)} %param.23) | copy-start | bytes 884740
  0.7 10.1 %copy-start.7 = (bf16[768,192]{0,1:T(8,128)(2,1)S(1)}, bf16[768,192]{0,1:T(8,128)(2,1)}, u32[]{:S(2)}) copy-start(bf16[768,192]{0,1:T(8,128)(2,1)} %param.22) | copy-start | bytes 884740
  13.7 112.0 %copy-start.4 = (s32[1024,2]{0,1:T(2,128)S(1)}, s32[1024,2]{0,1:T(2,128)}, u32[]{:S(2)}) copy-start(s32[1024,2]{0,1:T(2,128)} %param.33) | copy-start | bytes 24580
  125.7 1.4 copy-start
  168.1 1.1 copy-start.1
  169.3 1.1 copy-start.2
  170.4 0.6 copy-start.3
  352.3 10.2 %copy-start.10 = (f32[768,16]{0,1:T(8,128)}, f32[768,16]{0,1:T(8,128)S(1)}, u32[]{:S(2)}) copy-start(f32[768,16]{0,1:T(8,128)S(1)} %slice_bitcast_fusion.1) | copy-start | bytes 147460
  362.5 2.9 copy-start.6
  362.5 3.6 copy-start.5
